TPU v7x, 256 devices: a whole 4x4x8 slice. The times are simulated.
256 devices in a mesh: mon: 64 (over y, z, core), out: 4 (over x).
Axes of the slice: x: 4, y: 4, z: 8, core: 2. Of those that a mesh axis runs over, the one named last changes fastest.
Arguments:
- mon_flow: bfloat16 [24576, 128], P('mon'), may hold values from -2.5 to 2.5
- out_flow: bfloat16 [4, 4096, 128], P('out', 'mon'), may hold values from -2.5 to 2.5
- rating: float32 [24576], P('mon'), may hold values from 1 to 3
- weights: float32 [128], replicated, may hold values from 0.25 to 1
- lodf: bfloat16 [64, 4, 8, 128, 128], P('mon', 'out'), may hold values from -1 to 1
- tile_mon: int32 [64, 4, 8], P('mon', 'out'), may hold values from 0 to 2
- tile_out: int32 [64, 4, 8], P('mon', 'out'), may hold values from 0 to 31
- tile_count: int32 [64, 4], P('mon', 'out'), may hold values from 1 to 8, as said below
Outputs:
- grad_mon: float32 [24576, 128], P(('mon', 'out'))
- grad_out: float32 [4, 4096, 128], P('out', 'mon')
Inputs may be any that keep to these rules, and one draw needn't show every extreme that they name: `tile_count`: each device has 1 to 8 live slots; some device has exactly 8 in every draw.
All inputs are finite; a program needn't handle non-finite values.
Results may differ from a plain program's by a relative error of at most 0.00085.
Values may be sent and summed in bfloat16 or wider, within the bound.
A program may use at most 64 MiB of HBM per device.

v0:
```python
import jax
import jax.numpy as jnp
from jax import lax
from jax.sharding import PartitionSpec as P


def tile_grads(lodf_tile, mon_block, out_block, rating_rows, weights):
    coupling = lodf_tile.astype(jnp.float32)
    post_flow = (
        mon_block.astype(jnp.float32)[:, None, :]
        + coupling[:, :, None] * out_block.astype(jnp.float32)[None, :, :]
    )
    inverse = 1.0 / (rating_rows * rating_rows)
    excess = post_flow * post_flow * inverse[:, None, None] - 1.0
    derivative = jax.nn.softplus(excess) * jax.nn.sigmoid(excess) * post_flow
    derivative = (
        derivative * (4.0 / coupling.shape[0]) * inverse[:, None, None] * weights[None, None, :]
    )
    return (jnp.sum(derivative, axis=1), jnp.sum(coupling[:, :, None] * derivative, axis=0))


def local(mon_flow, out_flow, rating, weights, lodf, tile_mon, tile_out, tile_count):
    width = lodf.shape[-1]
    scen = mon_flow.shape[1]
    gathered = lax.all_gather(out_flow, "mon", axis=1, tiled=True)[0]
    outage_blocks = gathered.reshape(-1, width, scen)
    mon_start = jnp.zeros(mon_flow.shape, jnp.float32)
    out_start = jnp.zeros(outage_blocks.shape, jnp.float32)

    def one_tile(mon_part, lodf_tile, mon_index, out_block):
        start = mon_index * width
        mon_rows = lax.dynamic_slice_in_dim(mon_flow, start, width, 0)
        rating_rows = lax.dynamic_slice_in_dim(rating, start, width, 0)
        grad_m, grad_k = tile_grads(lodf_tile, mon_rows, out_block, rating_rows, weights)
        old_rows = lax.dynamic_slice_in_dim(mon_part, start, width, 0)
        return (lax.dynamic_update_slice_in_dim(mon_part, old_rows + grad_m, start, 0), grad_k)

    def own_tile(slot_index, totals):
        mon_part, out_part = totals
        out_index = tile_out[0, 0, slot_index]
        mon_part, grad_k = one_tile(
            mon_part, lodf[0, 0, slot_index], tile_mon[0, 0, slot_index], outage_blocks[out_index]
        )
        old_block = lax.dynamic_index_in_dim(out_part, out_index, 0, keepdims=False)
        out_part = lax.dynamic_update_index_in_dim(out_part, old_block + grad_k, out_index, 0)
        return (mon_part, out_part)

    own_count = tile_count[0, 0]
    mon_part, out_part = lax.fori_loop(0, own_count, own_tile, (mon_start, out_start))
    grad_mon = lax.psum_scatter(mon_part, "out", scatter_dimension=0, tiled=True)
    grad_out = lax.psum_scatter(
        out_part.reshape(1, -1, scen), "mon", scatter_dimension=1, tiled=True
    )
    return (grad_mon, grad_out)


def solution(mesh):
    in_specs = (
        P("mon", None),
        P("out", "mon", None),
        P("mon"),
        P(),
        P("mon", "out", None, None, None),
        P("mon", "out", None),
        P("mon", "out", None),
        P("mon", "out"),
    )
    out_specs = (P(("mon", "out"), None), P("out", "mon", None))
    return jax.shard_map(local, mesh=mesh, in_specs=in_specs, out_specs=out_specs, check_vma=False)
```

profile of v0, /device:TPU:1, one launch (start us, length us, event | category | flops | bytes accessed | tf_op | source)
XLA Modules:
  0.0 410.9 jit_solution(17934352737875300077)
XLA Ops:
  7.2 0.0 all-gather.2.cloned.1.call-start
  7.2 0.7 all-gather.2.cloned.1.call-update
  7.9 0.0 reduce-scatter.3.cloned.1.call-start
  8.0 83.5 %all-gather.2.cloned.1.call-done = bf16[1,4096,128]{2,1,0:T(8,128)(2,1)} async-done(((bf16[1,64,128]{2,1,0:T(8,128)(2,1)}), bf16[1,4096,128]{2,1,0:T(8,128)(2,1)}) %all-gather.2.cloned.1.call-update) | async-done | bytes 1048592 | tf_op jit(solution)/shard_map/all_gather | solution.py:25
  91.5 0.2 broadcast_in_dim.6
  91.8 38.2 %while.14 = (s32[]{:T(128)}, f32[384,128]{1,0:T(8,128)S(1)}, f32[32,128,128]{2,1,0:T(8,128)S(1)}, s32[]{:T(128)}, s32[1,1,8]{2,1,0:T(1,128)S(1)}, /*index=5*/bf1...) while((s32[]{:T(128)}, f32[384,128]{1,0:T(8,128)S(1)}, ...), condition=%wide.region_3.4_spmd, body=%wide.region_0.3_spmd.sunk | while | flops 44089740 | bytes 1019183 | solution.py:49
  92.4 0.6 constant_dynamic-slice_fusion.3
  96.9 0.8 broadcast_multiply_fusion.2
  97.6 0.8 bitcast_convert_fusion.4
  98.4 0.8 dynamic-slice_convert_fusion.2
  99.2 0.8 bitcast_convert_fusion.5
  99.9 10.5 %multiply_reduce_fusion.2 = (f32[128,128]{1,0:T(8,128)S(1)}, f32[128,128]{1,0:T(8,128)S(1)}) fusion(f32[128,128]{1,0:T(8,128)S(1)} %bitcast_convert_fusion.4, f32[128]{0:T(128)S(1)} %get-tuple-element.295, f32[128]{0:T(128)S(1)} %get-tuple-element.248, f32[128]{0:T(128)S(1)} %get-tuple-element.249, f32[128,128]{1,0:T(8,128)S(1)} %bitcast_convert_fusion.5, ...), kind=kLoop, calls=%fused_computation.5.clone.1 | loop fusion | flops 44007424 | bytes 329216 | tf_op jit(solution)/shard_map/while/body/reduce_sum | solution.py:19
  111.2 0.6 constant_dynamic-slice_fusion.3
  115.7 0.8 broadcast_multiply_fusion.2
  116.4 0.8 bitcast_convert_fusion.4
  117.2 0.8 dynamic-slice_convert_fusion.2
  118.0 0.8 bitcast_convert_fusion.5
  118.7 10.5 %multiply_reduce_fusion.2 = (f32[128,128]{1,0:T(8,128)S(1)}, f32[128,128]{1,0:T(8,128)S(1)}) fusion(f32[128,128]{1,0:T(8,128)S(1)} %bitcast_convert_fusion.4, f32[128]{0:T(128)S(1)} %get-tuple-element.295, f32[128]{0:T(128)S(1)} %get-tuple-element.248, f32[128]{0:T(128)S(1)} %get-tuple-element.249, f32[128,128]{1,0:T(8,128)S(1)} %bitcast_convert_fusion.5, ...), kind=kLoop, calls=%fused_computation.5.clone.1 | loop fusion | flops 44007424 | bytes 329216 | tf_op jit(solution)/shard_map/while/body/reduce_sum | solution.py:19
  130.0 0.6 copy-done.1
  130.7 0.0 reduce-scatter.5.cloned.1.call-start
  130.7 0.7 copy-done
  131.4 0.0 reduce-scatter.5.cloned.1.call-update
  131.4 130.1 %reduce-scatter.3.cloned.1.call-done = f32[96,128]{1,0:T(8,128)} async-done(((f32[384,128]{1,0:T(8,128)}), f32[96,128]{1,0:T(8,128)}) %reduce-scatter.3.cloned.1.call-update) | async-done | bytes 49168 | tf_op jit(solution)/shard_map/reduce_scatter | solution.py:50
  261.5 142.9 %reduce-scatter.5.cloned.1.call-done = f32[1,64,128]{2,1,0:T(8,128)} async-done(((f32[1,4096,128]{2,1,0:T(8,128)}), f32[1,64,128]{2,1,0:T(8,128)}) %reduce-scatter.5.cloned.1.call-update) | async-done | bytes 32784 | tf_op jit(solution)/shard_map/reduce_scatter | solution.py:51
  (14 shorter events, 0.1 us)
Async XLA Ops:
  7.2 84.6 %copy-start.3 = (s32[1,1,8]{2,1,0:T(1,128)S(1)}, s32[1,1,8]{2,1,0:T(1,128)}, u32[]{:S(2)}) copy-start(s32[1,1,8]{2,1,0:T(1,128)} %param.16) | copy-start | bytes 100
  7.2 84.6 %copy-start.2 = (s32[1,1,8]{2,1,0:T(1,128)S(1)}, s32[1,1,8]{2,1,0:T(1,128)}, u32[]{:S(2)}) copy-start(s32[1,1,8]{2,1,0:T(1,128)} %param.15) | copy-start | bytes 100
  7.2 84.6 %copy-start.4 = (f32[128]{0:T(128)S(1)}, f32[128]{0:T(128)}, u32[]{:S(2)}) copy-start(f32[128]{0:T(128)} %param.13) | copy-start | bytes 1540
  7.2 84.3 %all-gather.2.cloned.1.call-start = ((), (), s32[]{:S(2)}) async-start(), calls=%async_computation.2 | async-start | bytes 1064960 | tf_op jit(solution)/shard_map/all_gather | solution.py:25
  7.9 253.6 %reduce-scatter.3.cloned.1.call-start = ((), (), s32[]{:S(2)}) async-start(), calls=%async_computation.3 | async-start | bytes 245760 | tf_op jit(solution)/shard_map/reduce_scatter | solution.py:50
  130.0 0.7 copy-start.1
  130.0 1.4 copy-start
  130.7 273.7 %reduce-scatter.5.cloned.1.call-start = ((), (), s32[]{:S(2)}) async-start(), calls=%async_computation.4 | async-start | bytes 2129920 | tf_op jit(solution)/shard_map/reduce_scatter | solution.py:51
Sparse Core Ops, SparseCore 0:
  10.8 80.6 all-gather.1
  130.8 130.6 reduce-scatter.2
  266.7 137.6 reduce-scatter.4
where the time goes:
time: 418 us; the launch traced here: 411 us
  waiting for transfers between devices  357 us (85%)
  other arithmetic  28.5 us (7%)
  between operations  13.8 us (3%)
  loops' own time  9.73 us (2%)
    reduce_scatter x1, waiting for transfers between devices, local(): lax.psum_scatter(out_part.reshape(1, -1, scen), 'mon', scatter_dimension=...  143 us
    reduce_scatter x1, waiting for transfers between devices, local(): lax.psum_scatter(mon_part, 'out', scatter_dimension=0, tiled=True)  130 us
    all_gather x1, waiting for transfers between devices, local(): gathered = lax.all_gather(out_flow, 'mon', axis=1, tiled=True)[0]  83.5 us
    reduce_sum x2, other arithmetic, tile_grads(): jnp.sum(coupling[:, :, None] * derivative, axis=0)  21.1 us
    another operation x1, loops' own time, local(): lax.fori_loop(0, own_count, own_tile, (mon_start, out_start))  9.73 us
  transfers between devices with their start and end apart: 3, of which 3 were waited for; matrix products, arithmetic and copies ran while one was open for 0% of the time, Pallas kernels for 0%

commit v1 on v0

v1 whole, which is shorter than its diff:
```python
import functools
import math

import jax
import jax.numpy as jnp
from jax import lax
from jax.experimental import pallas as pl
from jax.experimental.pallas import tpu as pltpu
from jax.sharding import PartitionSpec as P

MESH = pl.DeviceIdType.MESH
NX, NY, NZ, NC = 4, 4, 8, 2
G = NX * NC
BLK = 128
S = 128
SLOTS = 8
KC = BLK // G
ROWS = BLK // NC // G
MB = 3
OWN = MB * BLK // NX
LOG2E = math.log2(math.e)
F32 = jnp.float32
BF16 = jnp.bfloat16


def position():
    i = lax.axis_index("mon")
    o = lax.axis_index("out")
    c = lax.rem(i, NC)
    z = lax.rem(i // NC, NZ)
    y = i // (NC * NZ)
    return o, y, z, c


def at(o, y, z, c):
    return ((y * NZ + z) * NC + c, o)


def peers(o, y, z, c):
    g = o * NC + c
    group = []
    for d in range(1, G):
        other = lax.rem(g + d, G)
        group.append((other, at(other // NC, y, z, lax.rem(other, NC))))
    along_z = []
    for d in range(1, NZ):
        other = lax.rem(z + d, NZ)
        along_z.append((other, at(o, y, other, c)))
    along_y = []
    for d in range(1, NY):
        other = lax.rem(y + d, NY)
        along_y.append((other, at(o, other, z, c)))
    return g, group, along_z, along_y


def signal_all(devices):
    barrier = pltpu.get_barrier_semaphore()
    for device in devices:
        pl.semaphore_signal(barrier, inc=1, device_id=device, device_id_type=MESH)


def send(src, dst, send_sem, recv_sem, device):
    copy = pltpu.make_async_remote_copy(
        src_ref=src, dst_ref=dst, send_sem=send_sem, recv_sem=recv_sem, device_id=device, device_id_type=MESH
    )
    copy.start()
    return copy


def gather_kernel(
    lodf_ref, flow_ref, rating_ref, mon_ref, meta_ref,
    tiles_ref, gathered_ref, mon_all_ref, small_ref, meta_all_ref,
    tiles_out, small_out, gs, gr, ms, mr, zs, zr, ys, yr,
):
    o, y, z, c = position()
    g, group, along_z, along_y = peers(o, y, z, c)
    signal_all([device for _, device in group + along_z + along_y])

    flow = flow_ref[...].astype(F32)
    small_out[...] = jnp.zeros_like(small_out)
    for m in range(G):
        small_out[m, 0:ROWS, :] = flow[m * ROWS : (m + 1) * ROWS, :]
        small_out[m, ROWS : ROWS + MB, :] = rating_ref[...]
    for q in range(SLOTS):
        turned = jnp.transpose(lodf_ref[q].astype(F32))
        for m in range(G):
            low = turned[m * ROWS : (m + 1) * ROWS, :]
            high = turned[BLK // 2 + m * ROWS : BLK // 2 + (m + 1) * ROWS, :]
            tiles_out[m, q] = jnp.concatenate([low, high], axis=0).astype(BF16)
    small_ref[g] = small_out[g]
    tiles_ref[g] = tiles_out[g]
    meta_all_ref[g] = meta_ref[...]
    mon_all_ref[c] = mon_ref[...]

    pl.semaphore_wait(pltpu.get_barrier_semaphore(), len(group) + len(along_z) + len(along_y))
    first = []
    rest = []
    for d, (other, device) in enumerate(group):
        first.append(send(small_out.at[other], small_ref.at[g], gs.at[0, d], gr.at[0, d], device))
    for d, (other, device) in enumerate(group):
        rest.append(send(meta_ref, meta_all_ref.at[g], gs.at[1, d], gr.at[1, d], device))
        rest.append(send(tiles_out.at[other], tiles_ref.at[g], gs.at[2, d], gr.at[2, d], device))
    rest.append(send(mon_ref, mon_all_ref.at[c], ms, mr, at(o, y, z, 1 - c)))
    for copy in first:
        copy.wait()
    block = jnp.concatenate([small_ref[m, 0:ROWS, :] for m in range(G)], axis=0).astype(BF16)
    mine = y * NZ + z
    gathered_ref[mine] = block
    hops = [
        send(gathered_ref.at[mine], gathered_ref.at[mine], zs.at[d], zr.at[d], device)
        for d, (_, device) in enumerate(along_z)
    ]
    for copy in hops:
        copy.wait()
    row = pl.ds(y * NZ, NZ)
    hops = [
        send(gathered_ref.at[row], gathered_ref.at[row], ys.at[d], yr.at[d], device)
        for d, (_, device) in enumerate(along_y)
    ]
    for copy in rest + hops:
        copy.wait()


def tile_kernel(
    meta_ref, tiles_ref, flow_ref, mon_ref, small_ref, weights_ref,
    grad_mon_ref, grad_out_ref,
    order, scaled, column, row_scale, spread, wide_a, wide_b, flow_rows,
):
    for c in range(NC):
        for t in range(MB):
            scale = math.sqrt(LOG2E) / small_ref[c, ROWS + t : ROWS + t + 1, :]
            row_scale[c * MB + t, :, :] = scale
            turned = jnp.transpose(jnp.broadcast_to(scale, (BLK, BLK)))
            column[pl.ds((c * MB + t) * BLK, BLK), :] = turned
            scaled[pl.ds((c * MB + t) * BLK, BLK), :] = turned * mon_ref[c, pl.ds(t * BLK, BLK), :].astype(F32)
    grad_mon_ref[...] = jnp.zeros_like(grad_mon_ref)
    grad_out_ref[...] = jnp.zeros_like(grad_out_ref)
    term = lax.broadcasted_iota(jnp.int32, spread.shape, 0)
    lane = lax.broadcasted_iota(jnp.int32, spread.shape, 1)
    spread[...] = jnp.where(lax.rem(term, KC) == lane // S, 1.0, 0.0).astype(BF16)

    def list_member(member, total):
        count = meta_ref[member, 0, 2 * SLOTS]

        def add(q, _):
            order[total + q] = member * SLOTS + q
            return 0

        lax.fori_loop(0, count, add, 0)
        return total + count

    total = lax.fori_loop(0, G, list_member, 0)

    def where_of(n):
        entry = order[jnp.minimum(n, total - 1)]
        member = entry // SLOTS
        return member, lax.rem(entry, SLOTS)

    def expand(n, wide):
        member, q = where_of(n)
        block = lax.rem(member, NC) * MB + meta_ref[member, 0, q]
        piece = tiles_ref[member, q].astype(F32) * row_scale[block]
        high = piece.astype(BF16)
        low = (piece - high.astype(F32)).astype(BF16)
        both = jnp.concatenate([high, low], axis=0)
        wide[...] = lax.dot_general(both, spread[...], (((0,), (0,)), ((), ())), preferred_element_type=F32)

    def work(n, wide, rows_at):
        member, q = where_of(n)
        block = lax.rem(member, NC) * MB + meta_ref[member, 0, q]
        outage = meta_ref[member, 0, SLOTS + q]
        start = pl.multiple_of(block * BLK, BLK)
        own = pl.ds(pl.multiple_of((member // NC) * KC, KC), KC)
        flow_rows[rows_at] = flow_ref[outage, own, :].astype(F32)
        for half in range(KC // 8):
            flows = [flow_rows[rows_at, pl.ds(half * 8 + j, 8, stride=0), :] for j in range(8)]
            sums = [None] * 8
            for i in range(BLK // 8):
                base = scaled[pl.ds(start + i * 8, 8), :]
                total_m = None
                for j in range(8):
                    factor = wide[pl.ds(i * 8, 8), pl.ds((half * 8 + j) * S, S)]
                    post = base + factor * flows[j]
                    square = post * post
                    level = jnp.log2(jnp.exp2(square) + math.e)
                    slope = (level - LOG2E) * jnp.exp2(square - level) * post
                    total_m = slope if total_m is None else total_m + slope
                    part = factor * slope
                    sums[j] = part if sums[j] is None else sums[j] + part
                grad_mon_ref[pl.ds(start + i * 8, 8), :] += total_m
            rows = jnp.concatenate([jnp.sum(v, axis=0, keepdims=True) for v in sums], axis=0)
            place = pl.ds(pl.multiple_of((member // NC) * KC + half * 8, 8), 8)
            grad_out_ref[outage, place, :] += rows

    expand(0, wide_a)

    def pair(p, _):
        expand(2 * p + 1, wide_b)
        work(2 * p, wide_a, 0)

        @pl.when(2 * p + 1 < total)
        def _():
            expand(2 * p + 2, wide_a)
            work(2 * p + 1, wide_b, 1)

        return 0

    lax.fori_loop(0, (total + 1) // 2, pair, 0)
    weight = weights_ref[...] * (4.0 / BLK * math.log(2.0) ** 2)
    grad_mon_ref[...] = grad_mon_ref[...] * column[...] * weight
    grad_out_ref[...] = grad_out_ref[...] * weight[None]


def scatter_kernel(
    mon_ref, flow_ref, grad_mon_ref, grad_out_ref,
    mon_in, y_in, y_sum, z_in, z_sum, last_in,
    gs, gr, fs, fr, zs, zr, ys, yr,
):
    o, y, z, c = position()
    g, group, along_z, along_y = peers(o, y, z, c)
    signal_all([device for _, device in group + along_z + along_y])
    pl.semaphore_wait(pltpu.get_barrier_semaphore(), len(group) + len(along_z) + len(along_y))

    hops_y = [
        send(flow_ref.at[pl.ds(other * NZ, NZ)], y_in.at[d], ys.at[d], yr.at[d], device)
        for d, (other, device) in enumerate(along_y)
    ]
    group_hops = []
    for d, (other, device) in enumerate(group):
        rows = pl.ds(pl.multiple_of(lax.rem(other, NC) * MB * BLK + (other // NC) * OWN, 8), OWN)
        group_hops.append(send(mon_ref.at[rows], mon_in.at[d], gs.at[d], gr.at[d], device))
    for copy in hops_y:
        copy.wait()
    y_sum[...] = (flow_ref[pl.ds(y * NZ, NZ)] + y_in[0]) + (y_in[1] + y_in[2])
    hops = [
        send(y_sum.at[other], z_in.at[d], zs.at[d], zr.at[d], device)
        for d, (other, device) in enumerate(along_z)
    ]
    for copy in group_hops:
        copy.wait()
    rows = pl.ds(pl.multiple_of(c * MB * BLK + o * OWN, 8), OWN)
    total = mon_ref[rows, :]
    for d in range(G - 1):
        total = total + mon_in[d]
    grad_mon_ref[...] = total
    for copy in hops:
        copy.wait()
    total = y_sum[z]
    for d in range(NZ - 1):
        total = total + z_in[d]
    for m in range(G):
        z_sum[m] = total[m * ROWS : (m + 1) * ROWS, :]
    last_in[g] = z_sum[g]
    hops = [
        send(z_sum.at[other], last_in.at[g], fs.at[d], fr.at[d], device)
        for d, (other, device) in enumerate(group)
    ]
    for copy in hops:
        copy.wait()
    for m in range(G):
        grad_out_ref[pl.ds(m * ROWS, ROWS), :] = last_in[m]


def vmem(count):
    return [pl.BlockSpec(memory_space=pltpu.VMEM)] * count


DMA = pltpu.SemaphoreType.DMA


def local(mon_flow, out_flow, rating, weights, lodf, tile_mon, tile_out, tile_count):
    blocks = NY * NZ
    meta = jnp.concatenate(
        [tile_mon[0], tile_out[0], tile_count, jnp.zeros((1, S - 2 * SLOTS - 1), jnp.int32)], axis=1
    )
    tiles, gathered, mon_all, small, meta_all = pl.pallas_call(
        gather_kernel,
        out_shape=(
            jax.ShapeDtypeStruct((G, SLOTS, KC, BLK), BF16),
            jax.ShapeDtypeStruct((blocks, G * ROWS, S), BF16),
            jax.ShapeDtypeStruct((NC, MB * BLK, S), BF16),
            jax.ShapeDtypeStruct((G, 2 * ROWS, S), F32),
            jax.ShapeDtypeStruct((G, 1, S), jnp.int32),
        ),
        in_specs=vmem(5),
        out_specs=tuple(vmem(5)),
        scratch_shapes=[
            pltpu.VMEM((G, SLOTS, KC, BLK), BF16),
            pltpu.VMEM((G, 2 * ROWS, S), F32),
            DMA((3, G - 1)), DMA((3, G - 1)), DMA, DMA,
            DMA((NZ - 1,)), DMA((NZ - 1,)), DMA((NY - 1,)), DMA((NY - 1,)),
        ],
        compiler_params=pltpu.CompilerParams(collective_id=0, has_side_effects=True),
        name="gather",
    )(lodf[0, 0], out_flow[0], rating.reshape(MB, BLK), mon_flow, meta)

    part_mon, part_out = pl.pallas_call(
        tile_kernel,
        out_shape=(
            jax.ShapeDtypeStruct((NC * MB * BLK, S), F32),
            jax.ShapeDtypeStruct((blocks, G * ROWS, S), F32),
        ),
        in_specs=[pl.BlockSpec(memory_space=pltpu.SMEM)] + vmem(5),
        out_specs=tuple(vmem(2)),
        scratch_shapes=[
            pltpu.SMEM((G * SLOTS,), jnp.int32),
            pltpu.VMEM((NC * MB * BLK, S), F32),
            pltpu.VMEM((NC * MB * BLK, S), F32),
            pltpu.VMEM((NC * MB, 1, BLK), F32),
            pltpu.VMEM((2 * KC, KC * S), BF16),
            pltpu.VMEM((BLK, KC * S), F32),
            pltpu.VMEM((BLK, KC * S), F32),
            pltpu.VMEM((2, KC, S), F32),
        ],
        compiler_params=pltpu.CompilerParams(vmem_limit_bytes=24 << 20),
        name="tiles",
    )(meta_all, tiles, gathered, mon_all, small, weights.reshape(1, S))

    grad_mon, grad_out = pl.pallas_call(
        scatter_kernel,
        out_shape=(
            jax.ShapeDtypeStruct((OWN, S), F32),
            jax.ShapeDtypeStruct((G * ROWS, S), F32),
        ),
        in_specs=vmem(2),
        out_specs=tuple(vmem(2)),
        scratch_shapes=[
            pltpu.VMEM((G - 1, OWN, S), F32),
            pltpu.VMEM((NY - 1, NZ, G * ROWS, S), F32),
            pltpu.VMEM((NZ, G * ROWS, S), F32),
            pltpu.VMEM((NZ - 1, G * ROWS, S), F32),
            pltpu.VMEM((G, ROWS, S), F32),
            pltpu.VMEM((G, ROWS, S), F32),
            DMA((G - 1,)), DMA((G - 1,)), DMA((G - 1,)), DMA((G - 1,)),
            DMA((NZ - 1,)), DMA((NZ - 1,)), DMA((NY - 1,)), DMA((NY - 1,)),
        ],
        compiler_params=pltpu.CompilerParams(
            collective_id=1, has_side_effects=True, vmem_limit_bytes=24 << 20
        ),
        name="scatter",
    )(part_mon, part_out)
    return grad_mon, grad_out[None]


def solution(mesh):
    in_specs = (
        P("mon", None),
        P("out", "mon", None),
        P("mon"),
        P(),
        P("mon", "out", None, None, None),
        P("mon", "out", None),
        P("mon", "out", None),
        P("mon", "out"),
    )
    out_specs = (P(("mon", "out"), None), P("out", "mon", None))
    return jax.shard_map(local, mesh=mesh, in_specs=in_specs, out_specs=out_specs, check_vma=False)
```

time: 418 us -> 93.3 us (0.22); the launches traced: 411 us -> 93 us
  waiting for transfers between devices: 357 us -> 0 us
  Pallas kernels: 0 us -> 84.8 us
  other arithmetic: 28.5 us -> 0.59 us
  between operations: 13.8 us -> 1.35 us
  loops' own time: 9.73 us -> 0 us
  local copies, waits for them, and re-layouts: 1.58 us -> 6.31 us
    reduce_scatter x2 -> x0, waiting for transfers between devices: 273 us -> none  [the longest x1 143 us: local(): lax.psum_scatter(out_part.reshape(1, -1, scen), 'mon', scatter_dimension=...]
    pallas_call x0 -> x3, Pallas kernels: none -> 84.8 us  [the longest x1 37.3 us: local(): pl.pallas_call(scatter_kernel, out_shape=(jax.ShapeDtypeStruct((OWN, S),...]
    all_gather x1 -> x0, waiting for transfers between devices: 83.5 us -> none  [local(): gathered = lax.all_gather(out_flow, 'mon', axis=1, tiled=True)[0]]
    reduce_sum x2 -> x0, other arithmetic: 21.1 us -> none  [tile_grads(): jnp.sum(coupling[:, :, None] * derivative, axis=0)]
    another operation x1 -> x0, loops' own time: 9.73 us -> none  [local(): lax.fori_loop(0, own_count, own_tile, (mon_start, out_start))]
    unnamed x10 -> x18, local copies, waits for them, and re-layouts: 1.34 us -> 6.31 us
  transfers between devices with their start and end apart: 3 -> 0, of which waited for: 3 -> 0; matrix products, arithmetic and copies ran while one was open for 0% -> 0% of each run, Pallas kernels for 0% -> 0%
where the time goes in v1:
time: 93.3 us; the launch traced here: 93 us
  Pallas kernels  84.8 us (91%)
  local copies, waits for them, and re-layouts  6.31 us (7%)
  between operations  1.35 us (1%)
    pallas_call x1, Pallas kernels, local(): pl.pallas_call(scatter_kernel, out_shape=(jax.ShapeDtypeStruct((OWN, S),...  37.3 us
    pallas_call x1, Pallas kernels, local(): pl.pallas_call(gather_kernel, out_shape=(jax.ShapeDtypeStruct((G, SLOTS,...  29.3 us
    pallas_call x1, Pallas kernels, local(): pl.pallas_call(tile_kernel, out_shape=(jax.ShapeDtypeStruct((NC * MB * BL...  18.2 us
    unnamed x18, local copies, waits for them, and re-layouts  6.31 us

profile of v1, /device:TPU:1, one launch (start us, length us, event | category | flops | bytes accessed | tf_op | source)
XLA Modules:
  0.0 93.0 jit_solution(17563849896543059036)
XLA Ops:
  1.3 0.0 copy-start.6
  1.3 0.0 copy-start.7
  1.3 0.6 copy-done.6
  1.9 0.0 copy-done.7
  1.9 0.6 bitcast_add_fusion.meta_ref
  2.5 29.3 %gather.1 = (bf16[8,8,16,128]{3,2,1,0:T(8,128)(2,1)}, bf16[32,64,128]{2,1,0:T(8,128)(2,1)}, bf16[2,384,128]{2,1,0:T(8,128)(2,1)}, f32[8,16,128]{2,1,0:T(8,128)}, s32[8,1,128]{2,1,0:T(1,128)}) custom-call(bf16[8,128,128]{2,1,0:T(8,128)(2,1)} %bitcast.11, bf16[64,128]{1,0:T(8,128)(2,1)} %bitcast.12, f32[3,128]{1,0:T(4,128)} %bitcast.13, ...), custom_call_target="tpu_custom_call" | custom-call | tf_op jit(solution)/shard_map/gather/pallas_call | solution.py:276
  31.8 0.0 copy-start.4
  31.9 0.0 copy-start.5
  31.9 0.7 copy-done.4
  32.5 0.0 copy-done.5
  32.5 0.0 copy-start
  32.5 1.0 %copy-done = bf16[32,64,128]{2,1,0:T(8,128)(2,1)S(1)} copy-done((bf16[32,64,128]{2,1,0:T(8,128)(2,1)S(1)}, bf16[32,64,128]{2,1,0:T(8,128)(2,1)}, u32[]{:S(2)}) %copy-start) | copy-done | bytes 524312
  33.6 0.0 copy-start.1
  33.6 0.9 %copy-done.1 = bf16[8,8,16,128]{3,2,1,0:T(8,128)(2,1)S(1)} copy-done((bf16[8,8,16,128]{3,2,1,0:T(8,128)(2,1)S(1)}, bf16[8,8,16,128]{3,2,1,0:T(8,128)(2,1)}, u32[]{:S(2)}) %copy-start.1) | copy-done | bytes 262168
  34.5 0.0 copy-start.2
  34.5 0.9 copy-done.2
  35.5 0.0 copy-start.3
  35.5 0.8 copy-done.3
  36.3 18.2 %tiles.1 = (f32[768,128]{1,0:T(8,128)S(1)}, f32[32,64,128]{2,1,0:T(8,128)S(1)}) custom-call(s32[8,1,128]{2,1,0:T(1,128)S(1)} %copy-done.4, bf16[8,8,16,128]{3,2,1,0:T(8,128)(2,1)S(1)} %copy-done.1, bf16[32,64,128]{2,1,0:T(8,128)(2,1)S(1)} %copy-done, bf16[2,384,128]{2,1,0:T(8,128)(2,1)S(1)} %copy-done.2, f32[8,16,128]{2,1,0:T(8,128)S(1)} %copy-done.3, ...), custom_call_target="tpu_custom_call" | custom-call | tf_op jit(solution)/shard_map/tiles/pallas_call | solution.py:297
  54.5 37.3 %scatter.1 = (f32[96,128]{1,0:T(8,128)S(1)}, f32[64,128]{1,0:T(8,128)S(1)}) custom-call(f32[768,128]{1,0:T(8,128)S(1)} %get-tuple-element.16.mon_ref, f32[32,64,128]{2,1,0:T(8,128)S(1)} %get-tuple-element.17.flow_ref), custom_call_target="tpu_custom_call" | custom-call | tf_op jit(solution)/shard_map/scatter/pallas_call | solution.py:319
  91.8 0.6 copy.13
  92.4 0.6 copy.14
  (1 shorter events, 0.0 us)
Async XLA Ops:
  1.3 0.7 copy-start.6
  1.3 0.7 copy-start.7
  31.8 0.7 copy-start.4
  31.9 0.7 copy-start.5
  32.5 1.0 %copy-start = (bf16[32,64,128]{2,1,0:T(8,128)(2,1)S(1)}, bf16[32,64,128]{2,1,0:T(8,128)(2,1)}, u32[]{:S(2)}) copy-start(bf16[32,64,128]{2,1,0:T(8,128)(2,1)} %get-tuple-element.13.flow_ref) | copy-start | bytes 1572868
  33.6 0.9 %copy-start.1 = (bf16[8,8,16,128]{3,2,1,0:T(8,128)(2,1)S(1)}, bf16[8,8,16,128]{3,2,1,0:T(8,128)(2,1)}, u32[]{:S(2)}) copy-start(bf16[8,8,16,128]{3,2,1,0:T(8,128)(2,1)} %get-tuple-element.12.tiles_ref) | copy-start | bytes 786436
  34.5 0.9 copy-start.2
  35.5 0.8 copy-start.3

commit v2 on v1

--- a/solution.py
+++ b/solution.py
@@ -19,6 +19,7 @@
 MB = 3
 OWN = MB * BLK // NX
 LOG2E = math.log2(math.e)
+VMEM_BYTES = 56 << 20
 F32 = jnp.float32
 BF16 = jnp.bfloat16
 
@@ -47,7 +48,7 @@
         other = lax.rem(z + d, NZ)
         along_z.append((other, at(o, y, other, c)))
     along_y = []
-    for d in range(1, NY):
+    for d in (1, NY - 1):
         other = lax.rem(y + d, NY)
         along_y.append((other, at(o, other, z, c)))
     return g, group, along_z, along_y
@@ -112,12 +113,24 @@
     ]
     for copy in hops:
         copy.wait()
-    row = pl.ds(y * NZ, NZ)
-    hops = [
-        send(gathered_ref.at[row], gathered_ref.at[row], ys.at[d], yr.at[d], device)
-        for d, (_, device) in enumerate(along_y)
-    ]
-    for copy in rest + hops:
+    up, down = at(o, lax.rem(y + 1, NY), z, c), at(o, lax.rem(y + NY - 1, NY), z, c)
+
+    def half(row, part):
+        return gathered_ref.at[pl.ds(lax.rem(row, NY) * NZ + part * (NZ // 2), NZ // 2)]
+
+    hops = []
+    for part in range(2):
+        own = half(y, part)
+        hops.append(send(own, own, ys.at[0, part], yr.at[0, part], up))
+        own = half(y, 1 - part)
+        hops.append(send(own, own, ys.at[1, part], yr.at[1, part], down))
+    hops[0].wait()
+    passed = half(y + NY - 1, 0)
+    hops.append(send(passed, passed, ys.at[0, 2], yr.at[0, 2], up))
+    hops[1].wait()
+    passed = half(y + 1, 1)
+    hops.append(send(passed, passed, ys.at[1, 2], yr.at[1, 2], down))
+    for copy in rest + hops[2:]:
         copy.wait()
 
 
@@ -213,7 +226,7 @@
 
 def scatter_kernel(
     mon_ref, flow_ref, grad_mon_ref, grad_out_ref,
-    mon_in, y_in, y_sum, z_in, z_sum, last_in,
+    mon_in, relay_in, relay_out, y_in, y_sum, z_in, z_sum, last_in,
     gs, gr, fs, fr, zs, zr, ys, yr,
 ):
     o, y, z, c = position()
@@ -221,17 +234,36 @@
     signal_all([device for _, device in group + along_z + along_y])
     pl.semaphore_wait(pltpu.get_barrier_semaphore(), len(group) + len(along_z) + len(along_y))
 
-    hops_y = [
-        send(flow_ref.at[pl.ds(other * NZ, NZ)], y_in.at[d], ys.at[d], yr.at[d], device)
-        for d, (other, device) in enumerate(along_y)
+    (up, up_device), (down, down_device) = along_y
+    far = lax.rem(y + 2, NY)
+    halfway = NZ // 2
+
+    def half(row, part):
+        return pl.ds(row * NZ + part * halfway, halfway)
+
+    relays = [
+        send(flow_ref.at[half(far, 0)], relay_in.at[0], ys.at[0], yr.at[0], up_device),
+        send(flow_ref.at[half(far, 1)], relay_in.at[1], ys.at[1], yr.at[1], down_device),
+    ]
+    plain = [
+        send(flow_ref.at[half(up, 1)], y_in.at[0, 1], ys.at[2], yr.at[2], up_device),
+        send(flow_ref.at[half(down, 0)], y_in.at[1, 0], ys.at[3], yr.at[3], down_device),
     ]
     group_hops = []
     for d, (other, device) in enumerate(group):
         rows = pl.ds(pl.multiple_of(lax.rem(other, NC) * MB * BLK + (other // NC) * OWN, 8), OWN)
         group_hops.append(send(mon_ref.at[rows], mon_in.at[d], gs.at[d], gr.at[d], device))
-    for copy in hops_y:
-        copy.wait()
-    y_sum[...] = (flow_ref[pl.ds(y * NZ, NZ)] + y_in[0]) + (y_in[1] + y_in[2])
+    relays[0].wait()
+    relay_out[0] = relay_in[0] + flow_ref[half(up, 0)]
+    plain.append(send(relay_out.at[0], y_in.at[0, 0], ys.at[4], yr.at[4], up_device))
+    relays[1].wait()
+    relay_out[1] = relay_in[1] + flow_ref[half(down, 1)]
+    plain.append(send(relay_out.at[1], y_in.at[1, 1], ys.at[5], yr.at[5], down_device))
+    for copy in plain:
+        copy.wait()
+    for part in range(2):
+        here = slice(part * halfway, (part + 1) * halfway)
+        y_sum[here] = flow_ref[half(y, part)] + y_in[0, part] + y_in[1, part]
     hops = [
         send(y_sum.at[other], z_in.at[d], zs.at[d], zr.at[d], device)
         for d, (other, device) in enumerate(along_z)
@@ -288,9 +320,9 @@
             pltpu.VMEM((G, SLOTS, KC, BLK), BF16),
             pltpu.VMEM((G, 2 * ROWS, S), F32),
             DMA((3, G - 1)), DMA((3, G - 1)), DMA, DMA,
-            DMA((NZ - 1,)), DMA((NZ - 1,)), DMA((NY - 1,)), DMA((NY - 1,)),
+            DMA((NZ - 1,)), DMA((NZ - 1,)), DMA((2, 3)), DMA((2, 3)),
         ],
-        compiler_params=pltpu.CompilerParams(collective_id=0, has_side_effects=True),
+        compiler_params=pltpu.CompilerParams(collective_id=0, has_side_effects=True, vmem_limit_bytes=VMEM_BYTES),
         name="gather",
     )(lodf[0, 0], out_flow[0], rating.reshape(MB, BLK), mon_flow, meta)
 
@@ -312,7 +344,7 @@
             pltpu.VMEM((BLK, KC * S), F32),
             pltpu.VMEM((2, KC, S), F32),
         ],
-        compiler_params=pltpu.CompilerParams(vmem_limit_bytes=24 << 20),
+        compiler_params=pltpu.CompilerParams(vmem_limit_bytes=VMEM_BYTES),
         name="tiles",
     )(meta_all, tiles, gathered, mon_all, small, weights.reshape(1, S))
 
@@ -326,16 +358,18 @@
         out_specs=tuple(vmem(2)),
         scratch_shapes=[
             pltpu.VMEM((G - 1, OWN, S), F32),
-            pltpu.VMEM((NY - 1, NZ, G * ROWS, S), F32),
+            pltpu.VMEM((2, NZ // 2, G * ROWS, S), F32),
+            pltpu.VMEM((2, NZ // 2, G * ROWS, S), F32),
+            pltpu.VMEM((2, 2, NZ // 2, G * ROWS, S), F32),
             pltpu.VMEM((NZ, G * ROWS, S), F32),
             pltpu.VMEM((NZ - 1, G * ROWS, S), F32),
             pltpu.VMEM((G, ROWS, S), F32),
             pltpu.VMEM((G, ROWS, S), F32),
             DMA((G - 1,)), DMA((G - 1,)), DMA((G - 1,)), DMA((G - 1,)),
-            DMA((NZ - 1,)), DMA((NZ - 1,)), DMA((NY - 1,)), DMA((NY - 1,)),
+            DMA((NZ - 1,)), DMA((NZ - 1,)), DMA((6,)), DMA((6,)),
         ],
         compiler_params=pltpu.CompilerParams(
-            collective_id=1, has_side_effects=True, vmem_limit_bytes=24 << 20
+            collective_id=1, has_side_effects=True, vmem_limit_bytes=VMEM_BYTES
         ),
         name="scatter",
     )(part_mon, part_out)

time: 93.3 us -> 90.4 us (0.969)
  local copies, waits for them, and re-layouts: 6.31 us -> 2.69 us
    unnamed x18 -> x8, local copies, waits for them, and re-layouts: 6.31 us -> 2.69 us
    pallas_call x1, Pallas kernels: 18.2 us -> 21.3 us  [local(): pl.pallas_call(tile_kernel, out_shape=(jax.ShapeDtypeStruct((NC * MB * BL...]
    pallas_call x1, Pallas kernels: 29.3 us -> 28 us  [local(): pl.pallas_call(gather_kernel, out_shape=(jax.ShapeDtypeStruct((G, SLOTS,...]
    pallas_call x1, Pallas kernels: 37.3 us -> 36.3 us  [local(): pl.pallas_call(scatter_kernel, out_shape=(jax.ShapeDtypeStruct((OWN, S),...]
where the time goes in v2:
time: 90.4 us; the launch traced here: 90.2 us
  Pallas kernels  85.6 us (95%)
  local copies, waits for them, and re-layouts  2.69 us (3%)
  between operations  1.33 us (1%)
    pallas_call x1, Pallas kernels, local(): pl.pallas_call(scatter_kernel, out_shape=(jax.ShapeDtypeStruct((OWN, S),...  36.3 us
    pallas_call x1, Pallas kernels, local(): pl.pallas_call(gather_kernel, out_shape=(jax.ShapeDtypeStruct((G, SLOTS,...  28 us
    pallas_call x1, Pallas kernels, local(): pl.pallas_call(tile_kernel, out_shape=(jax.ShapeDtypeStruct((NC * MB * BL...  21.3 us
    unnamed x8, local copies, waits for them, and re-layouts  2.69 us

profile of v2, /device:TPU:1, one launch (start us, length us, event | category | flops | bytes accessed | tf_op | source)
XLA Modules:
  0.0 90.2 jit_solution(6859731853644887062)
XLA Ops:
  1.3 0.0 copy-start.1
  1.3 0.0 copy-start.2
  1.3 0.6 copy-done.1
  1.9 0.0 copy-done.2
  1.9 0.6 bitcast_add_fusion.meta_ref
  2.5 28.0 %gather.1 = (bf16[8,8,16,128]{3,2,1,0:T(8,128)(2,1)}, bf16[32,64,128]{2,1,0:T(8,128)(2,1)}, bf16[2,384,128]{2,1,0:T(8,128)(2,1)}, f32[8,16,128]{2,1,0:T(8,128)}, s32[8,1,128]{2,1,0:T(1,128)}) custom-call(bf16[8,128,128]{2,1,0:T(8,128)(2,1)} %bitcast.9, bf16[64,128]{1,0:T(8,128)(2,1)} %bitcast.11, f32[3,128]{1,0:T(4,128)} %bitcast.12, ...), custom_call_target="tpu_custom_call" | custom-call | tf_op jit(solution)/shard_map/gather/pallas_call | solution.py:308
  30.5 21.3 %tiles.1 = (f32[768,128]{1,0:T(8,128)}, f32[32,64,128]{2,1,0:T(8,128)}) custom-call(s32[8,1,128]{2,1,0:T(1,128)} %get-tuple-element.11.meta_ref, bf16[8,8,16,128]{3,2,1,0:T(8,128)(2,1)} %get-tuple-element.12.tiles_ref, bf16[32,64,128]{2,1,0:T(8,128)(2,1)} %get-tuple-element.13.flow_ref, bf16[2,384,128]{2,1,0:T(8,128)(2,1)} %get-tuple-element.14.mon_ref, ...), custom_call_target="tpu_custom_call" | custom-call | tf_op jit(solution)/shard_map/tiles/pallas_call | solution.py:329
  51.8 36.3 %scatter.1 = (f32[96,128]{1,0:T(8,128)}, f32[64,128]{1,0:T(8,128)}) custom-call(f32[768,128]{1,0:T(8,128)} %get-tuple-element.16.mon_ref, f32[32,64,128]{2,1,0:T(8,128)} %get-tuple-element.17.flow_ref), custom_call_target="tpu_custom_call" | custom-call | tf_op jit(solution)/shard_map/scatter/pallas_call | solution.py:351
  88.1 0.0 copy-start
  88.2 1.4 %copy.13 = f32[96,128]{1,0:T(8,128)} copy(f32[96,128]{1,0:T(8,128)} %get-tuple-element.22) | data formatting | bytes 98304
  89.6 0.0 copy-done
  89.6 0.6 copy.14
  (1 shorter events, 0.0 us)
Async XLA Ops:
  1.3 0.7 copy-start.1
  1.3 0.7 copy-start.2
  88.1 1.4 %copy-start = (f32[64,128]{1,0:T(8,128)S(1)}, f32[64,128]{1,0:T(8,128)}, u32[]{:S(2)}) copy-start(f32[64,128]{1,0:T(8,128)} %get-tuple-element.19) | copy-start | bytes 98308

commit v3 on v0

v3 whole, which is shorter than its diff:
```python
import functools
import math

import jax
import jax.numpy as jnp
from jax import lax
from jax.experimental import pallas as pl
from jax.experimental.pallas import tpu as pltpu
from jax.sharding import PartitionSpec as P

MESH = pl.DeviceIdType.MESH
NX, NY, NZ, NC = 4, 4, 8, 2
NP = NY // 2
SAME = 2 * NX
G = SAME * NC
BLK = 128
S = 128
SLOTS = 8
KC = BLK // G
MB = 3
UNITS = 2 * NC * MB
SETS = NP * NZ * SAME
OWN = MB * BLK // NX
LOG2E = math.log2(math.e)
VMEM_BYTES = 56 << 20
F32 = jnp.float32
BF16 = jnp.bfloat16


def position():
    i = lax.axis_index("mon")
    o = lax.axis_index("out")
    c = lax.rem(i, NC)
    z = lax.rem(i // NC, NZ)
    y = i // (NC * NZ)
    p = y // 2
    return o, p, lax.rem(y + p, 2), z, c


def at(o, p, e, z, c):
    y = 2 * p + lax.rem(e + p, 2)
    return ((y * NZ + z) * NC + c, o)


def peers(o, p, e, z, c):
    own = (c * 2 + e) * NX + o
    group = []
    for d in range(1, G):
        other = lax.rem(own + d, G)
        oo, oe, oc = lax.rem(other, NX), lax.rem(other // NX, 2), other // SAME
        group.append((other, oo, oe, oc, at(oo, p, oe, z, oc)))
    same = []
    for d in range(1, SAME):
        other = lax.rem(e * NX + o + d, SAME)
        same.append((other, at(lax.rem(other, NX), p, other // NX, z, c)))
    along_z = {}
    for d in range(1, NZ):
        other = lax.rem(z + d, NZ)
        along_z[d] = (other, at(o, p, e, other, c))
    return own, group, same, along_z, at(o, 1 - p, e, z, c)


def enter(group, along_z, across):
    barrier = pltpu.get_barrier_semaphore()
    devices = [entry[-1] for entry in group] + [device for _, device in along_z.values()] + [across]
    for device in devices:
        pl.semaphore_signal(barrier, inc=1, device_id=device, device_id_type=MESH)
    return len(devices)


def send(src, dst, send_sem, recv_sem, device):
    copy = pltpu.make_async_remote_copy(
        src_ref=src, dst_ref=dst, send_sem=send_sem, recv_sem=recv_sem, device_id=device, device_id_type=MESH
    )
    copy.start()
    return copy


def gather_kernel(
    lodf_ref, flow_ref, rating_ref, mon_ref, meta_ref,
    tiles_ref, gathered_ref, mon_all_ref, rating_all_ref, meta_all_ref,
    tiles_out, flow_out, flow_in, gs, gr, fs, fr, ms, mr, zs, zr, ys, yr,
):
    o, p, e, z, c = position()
    own, group, same, along_z, across = peers(o, p, e, z, c)
    signals = enter(group, along_z, across)
    place = e * NX + o
    unit = e * NC + c
    flow_out[...] = flow_ref[...].astype(F32).reshape(SAME, KC, S)
    flow_in[place] = flow_out[place]
    for q in range(0, SLOTS, 2):
        first = jnp.transpose(lodf_ref[q].astype(F32))
        second = jnp.transpose(lodf_ref[q + 1].astype(F32))
        for m in range(G):
            rows = slice(m * KC, (m + 1) * KC)
            tiles_out[m, q * KC : (q + 2) * KC, :] = jnp.concatenate([first[rows], second[rows]], axis=0).astype(BF16)
    tiles_ref[own] = tiles_out[own]
    meta_all_ref[own] = meta_ref[...]
    mon_all_ref[unit] = mon_ref[...]
    rating_all_ref[unit] = rating_ref[...]

    pl.semaphore_wait(pltpu.get_barrier_semaphore(), signals)
    flows = [
        send(flow_out.at[other], flow_in.at[place], fs.at[d], fr.at[d], device)
        for d, (other, device) in enumerate(same)
    ]
    rest = []
    for d, (other, _, _, _, device) in enumerate(group):
        rest.append(send(tiles_out.at[other], tiles_ref.at[own], gs.at[0, d], gr.at[0, d], device))
    for d, (other, _, _, _, device) in enumerate(group):
        rest.append(send(meta_ref, meta_all_ref.at[own], gs.at[1, d], gr.at[1, d], device))
    for d in range(1, 2 * NC):
        other = lax.rem(unit + d, 2 * NC)
        device = at(o, p, other // NC, z, lax.rem(other, NC))
        rest.append(send(mon_ref, mon_all_ref.at[unit], ms.at[0, d - 1], mr.at[0, d - 1], device))
        rest.append(send(rating_ref, rating_all_ref.at[unit], ms.at[1, d - 1], mr.at[1, d - 1], device))
    for copy in flows:
        copy.wait()
    mine = p * NZ + z
    gathered_ref[mine] = flow_in[...].reshape(SAME * KC, S).astype(BF16)
    block = gathered_ref.at[mine]
    hops = {}
    for d in (4, 3, 5, 2, 6, 1, 7):
        hops[d] = send(block, block, zs.at[d - 1], zr.at[d - 1], along_z[d][1])
    crossed = [send(block, block, ys.at[0], yr.at[0], across)]
    for d in (1, 7, 2, 6, 3, 5, 4):
        hops[d].wait_recv()
        block = gathered_ref.at[p * NZ + lax.rem(z + NZ - d, NZ)]
        crossed.append(send(block, block, ys.at[d], yr.at[d], across))
    for copy in hops.values():
        copy.wait_send()
    for copy in rest + crossed:
        copy.wait()


def tile_kernel(
    meta_ref, tiles_ref, flow_ref, mon_ref, rating_ref, weights_ref,
    grad_mon_ref, grad_out_ref,
    from_list, block_list, set_list, scaled, column, row_scale, spread, pieces, flows, wide_a, wide_b,
):
    for u in range(2 * NC):
        for t in range(MB):
            b = u * MB + t
            scale = math.sqrt(LOG2E) / rating_ref[u, t : t + 1, :]
            row_scale[b, :, :] = scale
            turned = jnp.transpose(jnp.broadcast_to(scale, (BLK, BLK)))
            column[b * BLK : (b + 1) * BLK, :] = turned
            scaled[b * BLK : (b + 1) * BLK, :] = turned * mon_ref[u, t * BLK : (t + 1) * BLK, :].astype(F32)
    row_scale[UNITS, :, :] = jnp.zeros((1, BLK), F32)
    scaled[UNITS * BLK :, :] = jnp.zeros((BLK, S), F32)
    grad_mon_ref[...] = jnp.zeros_like(grad_mon_ref)
    grad_out_ref[...] = jnp.zeros_like(grad_out_ref)
    pieces[...] = tiles_ref[...].astype(F32).reshape(G * SLOTS, KC, BLK)
    flows[0:SETS] = flow_ref[...].astype(F32).reshape(SETS, KC, S)
    flows[SETS] = jnp.zeros((KC, S), F32)
    term = lax.broadcasted_iota(jnp.int32, spread.shape, 0)
    lane = lax.broadcasted_iota(jnp.int32, spread.shape, 1)
    spread[...] = jnp.where(lax.rem(term, KC) == lane // S, 1.0, 0.0).astype(BF16)

    def list_member(member, total):
        count = meta_ref[member, 0, 2 * SLOTS]
        unit = lax.rem(member // NX, 2) * NC + member // SAME
        out = lax.rem(member, NX)

        def add(q, _):
            block = meta_ref[member, 0, SLOTS + q]
            y = block // NZ
            p = y // 2
            row = (p * NZ + lax.rem(block, NZ)) * SAME + lax.rem(y + p, 2) * NX + out
            from_list[total + q] = member * SLOTS + q
            block_list[total + q] = unit * MB + meta_ref[member, 0, q]
            set_list[total + q] = row
            return 0

        lax.fori_loop(0, count, add, 0)
        return total + count

    total = lax.fori_loop(0, G, list_member, 0)
    for extra in range(3):
        from_list[total + extra] = 0
        block_list[total + extra] = UNITS
        set_list[total + extra] = SETS

    def expand(n, wide):
        piece = pieces[from_list[n]] * row_scale[block_list[n]]
        high = piece.astype(BF16).astype(F32)
        both = jnp.concatenate([high, piece - high], axis=0).astype(BF16)
        wide[...] = lax.dot_general(both, spread[...], (((0,), (0,)), ((), ())), preferred_element_type=F32)

    def work(n, wide):
        row = set_list[n]
        start = pl.multiple_of(block_list[n] * BLK, BLK)
        flow = [flows[row, pl.ds(j, 8, stride=0), :] for j in range(KC)]
        sums = [None] * KC
        for i in range(BLK // 8):
            base = scaled[pl.ds(start + i * 8, 8), :]
            total_m = None
            for j in range(KC):
                factor = wide[i * 8 : (i + 1) * 8, j * S : (j + 1) * S]
                post = base + factor * flow[j]
                square = post * post
                level = jnp.log2(jnp.exp2(square) + math.e)
                slope = (level - LOG2E) * jnp.exp2(square - level) * post
                total_m = slope if total_m is None else total_m + slope
                part = factor * slope
                sums[j] = part if sums[j] is None else sums[j] + part
            grad_mon_ref[pl.ds(start + i * 8, 8), :] += total_m
        grad_out_ref[row] += jnp.concatenate([jnp.sum(v, axis=0, keepdims=True) for v in sums], axis=0)

    expand(0, wide_a)

    def pair(n, _):
        expand(2 * n + 1, wide_b)
        work(2 * n, wide_a)
        expand(2 * n + 2, wide_a)
        work(2 * n + 1, wide_b)
        return 0

    lax.fori_loop(0, (total + 1) // 2, pair, 0)
    weight = weights_ref[...] * (4.0 / BLK * math.log(2.0) ** 2)
    grad_mon_ref[0 : UNITS * BLK, :] = grad_mon_ref[0 : UNITS * BLK, :] * column[...] * weight
    grad_out_ref[...] = grad_out_ref[...] * weight[None]


def scatter_kernel(
    mon_ref, flow_ref, grad_mon_ref, grad_out_ref,
    mon_in, y_in, y_sum, z_in, z_sum, last_in,
    gs, gr, fs, fr, zs, zr, ys, yr,
):
    o, p, e, z, c = position()
    own, group, same, along_z, across = peers(o, p, e, z, c)
    place = e * NX + o
    signals = enter(group, along_z, across)
    pl.semaphore_wait(pltpu.get_barrier_semaphore(), signals)

    order = (4, 3, 5, 2, 6, 1, 7, 0)
    crossed = {}
    for d in order:
        there = pl.ds(((1 - p) * NZ + lax.rem(z + d, NZ)) * SAME, SAME)
        crossed[d] = send(flow_ref.at[there], y_in.at[d], ys.at[d], yr.at[d], across)
    group_hops = []
    for d, (other, oo, oe, oc, device) in enumerate(group):
        rows = pl.ds(pl.multiple_of((oe * NC + oc) * MB * BLK + oo * OWN, 8), OWN)
        group_hops.append(send(mon_ref.at[rows], mon_in.at[d], gs.at[d], gr.at[d], device))
    hops = []
    for d in order:
        crossed[d].wait()
        here = pl.ds((p * NZ + lax.rem(z + d, NZ)) * SAME, SAME)
        y_sum[d] = flow_ref[here] + y_in[d]
        if d > 0:
            hops.append(send(y_sum.at[d], z_in.at[d - 1], zs.at[d - 1], zr.at[d - 1], along_z[d][1]))
    for copy in hops:
        copy.wait()
    total = y_sum[0]
    for d in range(NZ - 1):
        total = total + z_in[d]
    z_sum[...] = total
    last_in[place] = z_sum[place]
    hops = [
        send(z_sum.at[other], last_in.at[place], fs.at[d], fr.at[d], device)
        for d, (other, device) in enumerate(same)
    ]
    for copy in group_hops:
        copy.wait()
    rows = pl.ds(pl.multiple_of((e * NC + c) * MB * BLK + o * OWN, 8), OWN)
    total = mon_ref[rows, :]
    for d in range(G - 1):
        total = total + mon_in[d]
    grad_mon_ref[...] = total
    for copy in hops:
        copy.wait()
    for m in range(SAME):
        grad_out_ref[m * KC : (m + 1) * KC, :] = last_in[m]


def vmem(count):
    return [pl.BlockSpec(memory_space=pltpu.VMEM)] * count


DMA = pltpu.SemaphoreType.DMA


def local(mon_flow, out_flow, rating, weights, lodf, tile_mon, tile_out, tile_count):
    meta = jnp.concatenate(
        [tile_mon[0], tile_out[0], tile_count, jnp.zeros((1, S - 2 * SLOTS - 1), jnp.int32)], axis=1
    )
    tiles, gathered, mon_all, ratings, meta_all = pl.pallas_call(
        gather_kernel,
        out_shape=(
            jax.ShapeDtypeStruct((G, SLOTS * KC, BLK), BF16),
            jax.ShapeDtypeStruct((NP * NZ, SAME * KC, S), BF16),
            jax.ShapeDtypeStruct((2 * NC, MB * BLK, S), BF16),
            jax.ShapeDtypeStruct((2 * NC, MB, BLK), F32),
            jax.ShapeDtypeStruct((G, 1, S), jnp.int32),
        ),
        in_specs=vmem(5),
        out_specs=tuple(vmem(5)),
        scratch_shapes=[
            pltpu.VMEM((G, SLOTS * KC, BLK), BF16),
            pltpu.VMEM((SAME, KC, S), F32),
            pltpu.VMEM((SAME, KC, S), F32),
            DMA((2, G - 1)), DMA((2, G - 1)), DMA((SAME - 1,)), DMA((SAME - 1,)),
            DMA((2, 2 * NC - 1)), DMA((2, 2 * NC - 1)), DMA((NZ - 1,)), DMA((NZ - 1,)), DMA((NZ,)), DMA((NZ,)),
        ],
        compiler_params=pltpu.CompilerParams(collective_id=0, has_side_effects=True, vmem_limit_bytes=VMEM_BYTES),
        name="gather",
    )(lodf[0, 0], out_flow[0], rating.reshape(MB, BLK), mon_flow, meta)

    part_mon, part_out = pl.pallas_call(
        tile_kernel,
        out_shape=(
            jax.ShapeDtypeStruct(((UNITS + 1) * BLK, S), F32),
            jax.ShapeDtypeStruct((SETS + 1, KC, S), F32),
        ),
        in_specs=[pl.BlockSpec(memory_space=pltpu.SMEM)] + vmem(5),
        out_specs=tuple(vmem(2)),
        scratch_shapes=[
            pltpu.SMEM((G * SLOTS + 8,), jnp.int32),
            pltpu.SMEM((G * SLOTS + 8,), jnp.int32),
            pltpu.SMEM((G * SLOTS + 8,), jnp.int32),
            pltpu.VMEM(((UNITS + 1) * BLK, S), F32),
            pltpu.VMEM((UNITS * BLK, S), F32),
            pltpu.VMEM((UNITS + 1, 1, BLK), F32),
            pltpu.VMEM((2 * KC, KC * S), BF16),
            pltpu.VMEM((G * SLOTS, KC, BLK), F32),
            pltpu.VMEM((SETS + 1, KC, S), F32),
            pltpu.VMEM((BLK, KC * S), F32),
            pltpu.VMEM((BLK, KC * S), F32),
        ],
        compiler_params=pltpu.CompilerParams(vmem_limit_bytes=VMEM_BYTES),
        name="tiles",
    )(meta_all, tiles, gathered, mon_all, ratings, weights.reshape(1, S))

    grad_mon, grad_out = pl.pallas_call(
        scatter_kernel,
        out_shape=(
            jax.ShapeDtypeStruct((OWN, S), F32),
            jax.ShapeDtypeStruct((SAME * KC, S), F32),
        ),
        in_specs=vmem(2),
        out_specs=tuple(vmem(2)),
        scratch_shapes=[
            pltpu.VMEM((G - 1, OWN, S), F32),
            pltpu.VMEM((NZ, SAME, KC, S), F32),
            pltpu.VMEM((NZ, SAME, KC, S), F32),
            pltpu.VMEM((NZ - 1, SAME, KC, S), F32),
            pltpu.VMEM((SAME, KC, S), F32),
            pltpu.VMEM((SAME, KC, S), F32),
            DMA((G - 1,)), DMA((G - 1,)), DMA((SAME - 1,)), DMA((SAME - 1,)),
            DMA((NZ - 1,)), DMA((NZ - 1,)), DMA((NZ,)), DMA((NZ,)),
        ],
        compiler_params=pltpu.CompilerParams(
            collective_id=1, has_side_effects=True, vmem_limit_bytes=VMEM_BYTES
        ),
        name="scatter",
    )(part_mon, part_out)
    return grad_mon, grad_out[None]


def solution(mesh):
    in_specs = (
        P("mon", None),
        P("out", "mon", None),
        P("mon"),
        P(),
        P("mon", "out", None, None, None),
        P("mon", "out", None),
        P("mon", "out", None),
        P("mon", "out"),
    )
    out_specs = (P(("mon", "out"), None), P("out", "mon", None))
    return jax.shard_map(local, mesh=mesh, in_specs=in_specs, out_specs=out_specs, check_vma=False)
```

time: 418 us -> 79.4 us (0.19); the launches traced: 411 us -> 77.9 us
  waiting for transfers between devices: 357 us -> 0 us
  Pallas kernels: 0 us -> 73.3 us
  other arithmetic: 28.5 us -> 0.59 us
  between operations: 13.8 us -> 1.33 us
  loops' own time: 9.73 us -> 0 us
    reduce_scatter x2 -> x0, waiting for transfers between devices: 273 us -> none  [the longest x1 143 us: local(): lax.psum_scatter(out_part.reshape(1, -1, scen), 'mon', scatter_dimension=...]
    all_gather x1 -> x0, waiting for transfers between devices: 83.5 us -> none  [local(): gathered = lax.all_gather(out_flow, 'mon', axis=1, tiled=True)[0]]
    pallas_call x0 -> x3, Pallas kernels: none -> 73.3 us  [the longest x1 30.4 us: local(): pl.pallas_call(tile_kernel, out_shape=(jax.ShapeDtypeStruct(((UNITS + 1)...]
    reduce_sum x2 -> x0, other arithmetic: 21.1 us -> none  [tile_grads(): jnp.sum(coupling[:, :, None] * derivative, axis=0)]
    another operation x1 -> x0, loops' own time: 9.73 us -> none  [local(): lax.fori_loop(0, own_count, own_tile, (mon_start, out_start))]
  transfers between devices with their start and end apart: 3 -> 0, of which waited for: 3 -> 0; matrix products, arithmetic and copies ran while one was open for 0% -> 0% of each run, Pallas kernels for 0% -> 0%
where the time goes in v3:
time: 79.4 us; the launch traced here: 77.9 us
  Pallas kernels  73.3 us (92%)
  local copies, waits for them, and re-layouts  2.69 us (3%)
  between operations  1.33 us (2%)
    pallas_call x1, Pallas kernels, local(): pl.pallas_call(tile_kernel, out_shape=(jax.ShapeDtypeStruct(((UNITS + 1)...  30.4 us
    pallas_call x1, Pallas kernels, local(): pl.pallas_call(gather_kernel, out_shape=(jax.ShapeDtypeStruct((G, SLOTS *...  23.1 us
    pallas_call x1, Pallas kernels, local(): pl.pallas_call(scatter_kernel, out_shape=(jax.ShapeDtypeStruct((OWN, S),...  19.8 us
    unnamed x8, local copies, waits for them, and re-layouts  2.69 us

profile of v3, /device:TPU:1, one launch (start us, length us, event | category | flops | bytes accessed | tf_op | source)
XLA Modules:
  0.0 77.9 jit_solution(12388506395970853308)
XLA Ops:
  1.3 0.0 copy-start.1
  1.3 0.0 copy-start.2
  1.3 0.6 copy-done.1
  1.9 0.0 copy-done.2
  1.9 0.6 bitcast_add_fusion.meta_ref
  2.5 23.1 %gather.1 = (bf16[16,64,128]{2,1,0:T(8,128)(2,1)}, bf16[16,64,128]{2,1,0:T(8,128)(2,1)}, bf16[4,384,128]{2,1,0:T(8,128)(2,1)}, f32[4,3,128]{2,1,0:T(4,128)}, s32[16,1,128]{2,1,0:T(1,128)}) custom-call(bf16[8,128,128]{2,1,0:T(8,128)(2,1)} %bitcast.9, bf16[64,128]{1,0:T(8,128)(2,1)} %bitcast.11, f32[3,128]{1,0:T(4,128)} %bitcast.12, bf16[384,128]{1,0:T(8,128)(2,1)} %mon_ref.1, ...), custom_call_target="tpu_custom_call" | custom-call | tf_op jit(solution)/shard_map/gather/pallas_call | solution.py:287
  25.6 30.4 %tiles.1 = (f32[1664,128]{1,0:T(8,128)}, f32[129,8,128]{2,1,0:T(8,128)}) custom-call(s32[16,1,128]{2,1,0:T(1,128)} %get-tuple-element.11.meta_ref, bf16[16,64,128]{2,1,0:T(8,128)(2,1)} %get-tuple-element.12.tiles_ref, bf16[16,64,128]{2,1,0:T(8,128)(2,1)} %get-tuple-element.13.flow_ref, bf16[4,384,128]{2,1,0:T(8,128)(2,1)} %get-tuple-element.14.mon_ref, ...), custom_call_target="tpu_custom_call" | custom-call | tf_op jit(solution)/shard_map/tiles/pallas_call | solution.py:309
  56.0 19.8 %scatter.1 = (f32[96,128]{1,0:T(8,128)}, f32[64,128]{1,0:T(8,128)}) custom-call(f32[1664,128]{1,0:T(8,128)} %get-tuple-element.16.mon_ref, f32[129,8,128]{2,1,0:T(8,128)} %get-tuple-element.17.flow_ref), custom_call_target="tpu_custom_call" | custom-call | tf_op jit(solution)/shard_map/scatter/pallas_call | solution.py:334
  75.9 0.0 copy-start
  75.9 1.4 %copy.13 = f32[96,128]{1,0:T(8,128)} copy(f32[96,128]{1,0:T(8,128)} %get-tuple-element.22) | data formatting | bytes 98304
  77.3 0.0 copy-done
  77.3 0.6 copy.14
  (1 shorter events, 0.0 us)
Async XLA Ops:
  1.3 0.7 copy-start.1
  1.3 0.7 copy-start.2
  75.9 1.4 %copy-start = (f32[64,128]{1,0:T(8,128)S(1)}, f32[64,128]{1,0:T(8,128)}, u32[]{:S(2)}) copy-start(f32[64,128]{1,0:T(8,128)} %get-tuple-element.19) | copy-start | bytes 98308

commit v4 on v3

--- a/solution.py
+++ b/solution.py
@@ -22,7 +22,7 @@
 SETS = NP * NZ * SAME
 OWN = MB * BLK // NX
 LOG2E = math.log2(math.e)
-VMEM_BYTES = 56 << 20
+VMEM_BYTES = 16 << 20
 F32 = jnp.float32
 BF16 = jnp.bfloat16
 
@@ -77,17 +77,41 @@
 
 
 def gather_kernel(
-    lodf_ref, flow_ref, rating_ref, mon_ref, meta_ref,
+    count_ref, tile_mon_hbm, tile_out_hbm, lodf_hbm, flow_hbm, rating_hbm, mon_hbm,
     tiles_ref, gathered_ref, mon_all_ref, rating_all_ref, meta_all_ref,
-    tiles_out, flow_out, flow_in, gs, gr, fs, fr, ms, mr, zs, zr, ys, yr,
+    tile_mon_ref, tile_out_ref, lodf_ref, flow_ref, tiles_out, flow_out, flow_in, loads, gs, gr, fs, fr, ms, mr, zs, zr, ys, yr,
 ):
     o, p, e, z, c = position()
+    place = e * NX + o
+    unit = e * NC + c
+    load_flow = pltpu.make_async_copy(flow_hbm, flow_ref, loads.at[0])
+    load_lodf = pltpu.make_async_copy(lodf_hbm, lodf_ref, loads.at[1])
+    load_mon = pltpu.make_async_copy(mon_hbm, mon_all_ref.at[unit], loads.at[2])
+    load_rating = pltpu.make_async_copy(rating_hbm, rating_all_ref.at[unit], loads.at[3])
+    words_in = [
+        pltpu.make_async_copy(tile_mon_hbm, tile_mon_ref, loads.at[4]),
+        pltpu.make_async_copy(tile_out_hbm, tile_out_ref, loads.at[5]),
+    ]
+    for load in [load_flow, load_lodf, load_mon, load_rating] + words_in:
+        load.start()
     own, group, same, along_z, across = peers(o, p, e, z, c)
     signals = enter(group, along_z, across)
-    place = e * NX + o
-    unit = e * NC + c
+    for load in words_in:
+        load.wait()
+    lane = lax.broadcasted_iota(jnp.int32, (1, S), 1)
+    words = jnp.where(lane == 2 * SLOTS, count_ref[0, 0], 0)
+    for q in range(SLOTS):
+        block = tile_out_ref[0, q]
+        across_y = block // NZ
+        pair = across_y // 2
+        row = (pair * NZ + lax.rem(block, NZ)) * SAME + lax.rem(across_y + pair, 2) * NX + o
+        words = jnp.where(lane == q, unit * MB + tile_mon_ref[0, q], words)
+        words = jnp.where(lane == SLOTS + q, row, words)
+    meta_all_ref[own] = words
+    load_flow.wait()
     flow_out[...] = flow_ref[...].astype(F32).reshape(SAME, KC, S)
     flow_in[place] = flow_out[place]
+    load_lodf.wait()
     for q in range(0, SLOTS, 2):
         first = jnp.transpose(lodf_ref[q].astype(F32))
         second = jnp.transpose(lodf_ref[q + 1].astype(F32))
@@ -95,9 +119,8 @@
             rows = slice(m * KC, (m + 1) * KC)
             tiles_out[m, q * KC : (q + 2) * KC, :] = jnp.concatenate([first[rows], second[rows]], axis=0).astype(BF16)
     tiles_ref[own] = tiles_out[own]
-    meta_all_ref[own] = meta_ref[...]
-    mon_all_ref[unit] = mon_ref[...]
-    rating_all_ref[unit] = rating_ref[...]
+    load_mon.wait()
+    load_rating.wait()
 
     pl.semaphore_wait(pltpu.get_barrier_semaphore(), signals)
     flows = [
@@ -108,12 +131,12 @@
     for d, (other, _, _, _, device) in enumerate(group):
         rest.append(send(tiles_out.at[other], tiles_ref.at[own], gs.at[0, d], gr.at[0, d], device))
     for d, (other, _, _, _, device) in enumerate(group):
-        rest.append(send(meta_ref, meta_all_ref.at[own], gs.at[1, d], gr.at[1, d], device))
+        rest.append(send(meta_all_ref.at[own], meta_all_ref.at[own], gs.at[1, d], gr.at[1, d], device))
     for d in range(1, 2 * NC):
         other = lax.rem(unit + d, 2 * NC)
         device = at(o, p, other // NC, z, lax.rem(other, NC))
-        rest.append(send(mon_ref, mon_all_ref.at[unit], ms.at[0, d - 1], mr.at[0, d - 1], device))
-        rest.append(send(rating_ref, rating_all_ref.at[unit], ms.at[1, d - 1], mr.at[1, d - 1], device))
+        rest.append(send(mon_all_ref.at[unit], mon_all_ref.at[unit], ms.at[0, d - 1], mr.at[0, d - 1], device))
+        rest.append(send(rating_all_ref.at[unit], rating_all_ref.at[unit], ms.at[1, d - 1], mr.at[1, d - 1], device))
     for copy in flows:
         copy.wait()
     mine = p * NZ + z
@@ -134,10 +157,12 @@
 
 
 def tile_kernel(
-    meta_ref, tiles_ref, flow_ref, mon_ref, rating_ref, weights_ref,
+    meta_ref, tiles_ref, flow_ref, mon_ref, rating_ref, weights_hbm,
     grad_mon_ref, grad_out_ref,
-    from_list, block_list, set_list, scaled, column, row_scale, spread, pieces, flows, wide_a, wide_b,
+    from_list, block_list, set_list, weights_ref, load, scaled, column, row_scale, spread, pieces, flows, wide_a, wide_b,
 ):
+    load_weights = pltpu.make_async_copy(weights_hbm, weights_ref, load)
+    load_weights.start()
     for u in range(2 * NC):
         for t in range(MB):
             b = u * MB + t
@@ -159,17 +184,11 @@
 
     def list_member(member, total):
         count = meta_ref[member, 0, 2 * SLOTS]
-        unit = lax.rem(member // NX, 2) * NC + member // SAME
-        out = lax.rem(member, NX)
 
         def add(q, _):
-            block = meta_ref[member, 0, SLOTS + q]
-            y = block // NZ
-            p = y // 2
-            row = (p * NZ + lax.rem(block, NZ)) * SAME + lax.rem(y + p, 2) * NX + out
             from_list[total + q] = member * SLOTS + q
-            block_list[total + q] = unit * MB + meta_ref[member, 0, q]
-            set_list[total + q] = row
+            block_list[total + q] = meta_ref[member, 0, q]
+            set_list[total + q] = meta_ref[member, 0, SLOTS + q]
             return 0
 
         lax.fori_loop(0, count, add, 0)
@@ -217,6 +236,7 @@
         return 0
 
     lax.fori_loop(0, (total + 1) // 2, pair, 0)
+    load_weights.wait()
     weight = weights_ref[...] * (4.0 / BLK * math.log(2.0) ** 2)
     grad_mon_ref[0 : UNITS * BLK, :] = grad_mon_ref[0 : UNITS * BLK, :] * column[...] * weight
     grad_out_ref[...] = grad_out_ref[...] * weight[None]
@@ -281,9 +301,11 @@
 
 
 def local(mon_flow, out_flow, rating, weights, lodf, tile_mon, tile_out, tile_count):
-    meta = jnp.concatenate(
-        [tile_mon[0], tile_out[0], tile_count, jnp.zeros((1, S - 2 * SLOTS - 1), jnp.int32)], axis=1
-    )
+    inputs = [
+        tile_mon[0], tile_out[0],
+        lodf[0, 0], out_flow[0], rating.reshape(MB, BLK), mon_flow, weights.reshape(1, S),
+    ]
+    inputs = [pltpu.with_memory_space_constraint(x, pltpu.HBM) for x in inputs]
     tiles, gathered, mon_all, ratings, meta_all = pl.pallas_call(
         gather_kernel,
         out_shape=(
@@ -293,18 +315,22 @@
             jax.ShapeDtypeStruct((2 * NC, MB, BLK), F32),
             jax.ShapeDtypeStruct((G, 1, S), jnp.int32),
         ),
-        in_specs=vmem(5),
+        in_specs=[pl.BlockSpec(memory_space=pltpu.SMEM)] + [pl.BlockSpec(memory_space=pltpu.HBM)] * 6,
         out_specs=tuple(vmem(5)),
         scratch_shapes=[
+            pltpu.SMEM((1, SLOTS), jnp.int32),
+            pltpu.SMEM((1, SLOTS), jnp.int32),
+            pltpu.VMEM((SLOTS, BLK, BLK), BF16),
+            pltpu.VMEM((SAME * KC, S), BF16),
             pltpu.VMEM((G, SLOTS * KC, BLK), BF16),
             pltpu.VMEM((SAME, KC, S), F32),
             pltpu.VMEM((SAME, KC, S), F32),
-            DMA((2, G - 1)), DMA((2, G - 1)), DMA((SAME - 1,)), DMA((SAME - 1,)),
+            DMA((6,)), DMA((2, G - 1)), DMA((2, G - 1)), DMA((SAME - 1,)), DMA((SAME - 1,)),
             DMA((2, 2 * NC - 1)), DMA((2, 2 * NC - 1)), DMA((NZ - 1,)), DMA((NZ - 1,)), DMA((NZ,)), DMA((NZ,)),
         ],
         compiler_params=pltpu.CompilerParams(collective_id=0, has_side_effects=True, vmem_limit_bytes=VMEM_BYTES),
         name="gather",
-    )(lodf[0, 0], out_flow[0], rating.reshape(MB, BLK), mon_flow, meta)
+    )(tile_count, *inputs[:6])
 
     part_mon, part_out = pl.pallas_call(
         tile_kernel,
@@ -312,12 +338,14 @@
             jax.ShapeDtypeStruct(((UNITS + 1) * BLK, S), F32),
             jax.ShapeDtypeStruct((SETS + 1, KC, S), F32),
         ),
-        in_specs=[pl.BlockSpec(memory_space=pltpu.SMEM)] + vmem(5),
+        in_specs=[pl.BlockSpec(memory_space=pltpu.SMEM)] + vmem(4) + [pl.BlockSpec(memory_space=pltpu.HBM)],
         out_specs=tuple(vmem(2)),
         scratch_shapes=[
             pltpu.SMEM((G * SLOTS + 8,), jnp.int32),
             pltpu.SMEM((G * SLOTS + 8,), jnp.int32),
             pltpu.SMEM((G * SLOTS + 8,), jnp.int32),
+            pltpu.VMEM((1, S), F32),
+            DMA,
             pltpu.VMEM(((UNITS + 1) * BLK, S), F32),
             pltpu.VMEM((UNITS * BLK, S), F32),
             pltpu.VMEM((UNITS + 1, 1, BLK), F32),
@@ -329,7 +357,7 @@
         ],
         compiler_params=pltpu.CompilerParams(vmem_limit_bytes=VMEM_BYTES),
         name="tiles",
-    )(meta_all, tiles, gathered, mon_all, ratings, weights.reshape(1, S))
+    )(meta_all, tiles, gathered, mon_all, ratings, inputs[6])
 
     grad_mon, grad_out = pl.pallas_call(
         scatter_kernel,

time: 79.4 us -> 69.5 us (0.88)
  Pallas kernels: 73.3 us -> 66.2 us
  local copies, waits for them, and re-layouts: 2.69 us -> 1.24 us
    pallas_call x1, Pallas kernels: 30.4 us -> 19.3 us  [local(): pl.pallas_call(tile_kernel, out_shape=(jax.ShapeDtypeStruct(((UNITS + 1)...]
    pallas_call x1, Pallas kernels: 19.8 us -> 25 us  [local(): pl.pallas_call(scatter_kernel, out_shape=(jax.ShapeDtypeStruct((OWN, S),...]
    unnamed x8 -> x2, local copies, waits for them, and re-layouts: 2.69 us -> 1.24 us
    pallas_call x1, Pallas kernels: 23.1 us -> 21.8 us  [local(): pl.pallas_call(gather_kernel, out_shape=(jax.ShapeDtypeStruct((G, SLOTS *...]
where the time goes in v4:
time: 69.5 us; the launch traced here: 68.7 us
  Pallas kernels  66.2 us (95%)
  between operations  1.3 us (2%)
  local copies, waits for them, and re-layouts  1.24 us (2%)
    pallas_call x1, Pallas kernels, local(): pl.pallas_call(scatter_kernel, out_shape=(jax.ShapeDtypeStruct((OWN, S),...  25 us
    pallas_call x1, Pallas kernels, local(): pl.pallas_call(gather_kernel, out_shape=(jax.ShapeDtypeStruct((G, SLOTS *...  21.8 us
    pallas_call x1, Pallas kernels, local(): pl.pallas_call(tile_kernel, out_shape=(jax.ShapeDtypeStruct(((UNITS + 1)...  19.3 us

profile of v4, /device:TPU:1, one launch (start us, length us, event | category | flops | bytes accessed | tf_op | source)
XLA Modules:
  0.0 68.7 jit_solution(6431466715317598881)
XLA Ops:
  1.3 21.8 %gather.1 = (bf16[16,64,128]{2,1,0:T(8,128)(2,1)S(1)}, bf16[16,64,128]{2,1,0:T(8,128)(2,1)S(1)}, bf16[4,384,128]{2,1,0:T(8,128)(2,1)S(1)}, f32[4,3,128]{2,1,0:T(4,128)S(1)}, s32[16,1,128]{2,1,0:T(1,128)S(1)}) custom-call(s32[1,1]{1,0:T(1,128)S(6)} %copy.12.count_ref, s32[1,8]{1,0:T(1,128)} %bitcast.11, s32[1,8]{1,0:T(1,128)} %bitcast.12, ...), custom_call_target="tpu_custom_call" | custom-call | tf_op jit(solution)/shard_map/gather/pallas_call | solution.py:309
  23.1 19.3 %tiles.1 = (f32[1664,128]{1,0:T(8,128)S(1)}, f32[129,8,128]{2,1,0:T(8,128)S(1)}) custom-call(s32[16,1,128]{2,1,0:T(1,128)S(1)} %get-tuple-element.11.meta_ref, bf16[16,64,128]{2,1,0:T(8,128)(2,1)S(1)} %get-tuple-element.12.tiles_ref, bf16[16,64,128]{2,1,0:T(8,128)(2,1)S(1)} %get-tuple-element.13.flow_ref, ...), custom_call_target="tpu_custom_call" | custom-call | tf_op jit(solution)/shard_map/tiles/pallas_call | solution.py:335
  42.4 25.0 %scatter.1 = (f32[96,128]{1,0:T(8,128)S(1)}, f32[64,128]{1,0:T(8,128)S(1)}) custom-call(f32[1664,128]{1,0:T(8,128)S(1)} %get-tuple-element.16.mon_ref, f32[129,8,128]{2,1,0:T(8,128)S(1)} %get-tuple-element.17.flow_ref), custom_call_target="tpu_custom_call" | custom-call | tf_op jit(solution)/shard_map/scatter/pallas_call | solution.py:362
  67.5 0.6 copy.13
  68.1 0.6 copy.14

commit v5 on v4

--- a/solution.py
+++ b/solution.py
@@ -18,6 +18,7 @@
 SLOTS = 8
 KC = BLK // G
 MB = 3
+UNROLL = 8
 UNITS = 2 * NC * MB
 SETS = NP * NZ * SAME
 OWN = MB * BLK // NX
@@ -228,14 +229,18 @@
 
     expand(0, wide_a)
 
-    def pair(n, _):
-        expand(2 * n + 1, wide_b)
-        work(2 * n, wide_a)
-        expand(2 * n + 2, wide_a)
-        work(2 * n + 1, wide_b)
+    def steps(first, count):
+        for k in range(0, count, 2):
+            expand(first + k + 1, wide_b)
+            work(first + k, wide_a)
+            expand(first + k + 2, wide_a)
+            work(first + k + 1, wide_b)
         return 0
 
-    lax.fori_loop(0, (total + 1) // 2, pair, 0)
+    long = total // UNROLL
+    lax.fori_loop(0, long, lambda n, _: steps(n * UNROLL, UNROLL), 0)
+    done = long * UNROLL
+    lax.fori_loop(0, (total - done + 1) // 2, lambda n, _: steps(done + 2 * n, 2), 0)
     load_weights.wait()
     weight = weights_ref[...] * (4.0 / BLK * math.log(2.0) ** 2)
     grad_mon_ref[0 : UNITS * BLK, :] = grad_mon_ref[0 : UNITS * BLK, :] * column[...] * weight

time: 69.5 us -> 63.7 us (0.917)
  Pallas kernels: 66.2 us -> 60.8 us
    pallas_call x1, Pallas kernels: 25 us -> 19.3 us  [local(): pl.pallas_call(scatter_kernel, out_shape=(jax.ShapeDtypeStruct((OWN, S),...]
where the time goes in v5:
time: 63.7 us; the launch traced here: 63.3 us
  Pallas kernels  60.8 us (95%)
  between operations  1.3 us (2%)
  local copies, waits for them, and re-layouts  1.24 us (2%)
    pallas_call x1, Pallas kernels, local(): pl.pallas_call(gather_kernel, out_shape=(jax.ShapeDtypeStruct((G, SLOTS *...  21.8 us
    pallas_call x1, Pallas kernels, local(): pl.pallas_call(tile_kernel, out_shape=(jax.ShapeDtypeStruct(((UNITS + 1)...  19.6 us
    pallas_call x1, Pallas kernels, local(): pl.pallas_call(scatter_kernel, out_shape=(jax.ShapeDtypeStruct((OWN, S),...  19.3 us

profile of v5, /device:TPU:1, one launch (start us, length us, event | category | flops | bytes accessed | tf_op | source)
XLA Modules:
  0.0 63.3 jit_solution(14307570998951323893)
XLA Ops:
  1.3 21.8 %gather.1 = (bf16[16,64,128]{2,1,0:T(8,128)(2,1)S(1)}, bf16[16,64,128]{2,1,0:T(8,128)(2,1)S(1)}, bf16[4,384,128]{2,1,0:T(8,128)(2,1)S(1)}, f32[4,3,128]{2,1,0:T(4,128)S(1)}, s32[16,1,128]{2,1,0:T(1,128)S(1)}) custom-call(s32[1,1]{1,0:T(1,128)S(6)} %copy.12.count_ref, s32[1,8]{1,0:T(1,128)} %bitcast.11, s32[1,8]{1,0:T(1,128)} %bitcast.12, ...), custom_call_target="tpu_custom_call" | custom-call | tf_op jit(solution)/shard_map/gather/pallas_call | solution.py:314
  23.1 19.6 %tiles.1 = (f32[1664,128]{1,0:T(8,128)S(1)}, f32[129,8,128]{2,1,0:T(8,128)S(1)}) custom-call(s32[16,1,128]{2,1,0:T(1,128)S(1)} %get-tuple-element.11.meta_ref, bf16[16,64,128]{2,1,0:T(8,128)(2,1)S(1)} %get-tuple-element.12.tiles_ref, bf16[16,64,128]{2,1,0:T(8,128)(2,1)S(1)} %get-tuple-element.13.flow_ref, ...), custom_call_target="tpu_custom_call" | custom-call | tf_op jit(solution)/shard_map/tiles/pallas_call | solution.py:340
  42.7 19.3 %scatter.1 = (f32[96,128]{1,0:T(8,128)S(1)}, f32[64,128]{1,0:T(8,128)S(1)}) custom-call(f32[1664,128]{1,0:T(8,128)S(1)} %get-tuple-element.16.mon_ref, f32[129,8,128]{2,1,0:T(8,128)S(1)} %get-tuple-element.17.flow_ref), custom_call_target="tpu_custom_call" | custom-call | tf_op jit(solution)/shard_map/scatter/pallas_call | solution.py:367
  62.1 0.6 copy.13
  62.7 0.6 copy.14

commit v6 on v5

--- a/solution.py
+++ b/solution.py
@@ -158,12 +158,14 @@
 
 
 def tile_kernel(
-    meta_ref, tiles_ref, flow_ref, mon_ref, rating_ref, weights_hbm,
+    words_ref, tiles_ref, flow_ref, mon_ref, rating_ref, weights_hbm,
     grad_mon_ref, grad_out_ref,
-    from_list, block_list, set_list, weights_ref, load, scaled, column, row_scale, spread, pieces, flows, wide_a, wide_b,
+    meta_ref, from_list, block_list, set_list, weights_ref, load, load_words, scaled, column, row_scale, spread, pieces, flows, wide_a, wide_b,
 ):
     load_weights = pltpu.make_async_copy(weights_hbm, weights_ref, load)
     load_weights.start()
+    words = pltpu.make_async_copy(words_ref, meta_ref, load_words)
+    words.start()
     for u in range(2 * NC):
         for t in range(MB):
             b = u * MB + t
@@ -182,6 +184,8 @@
     term = lax.broadcasted_iota(jnp.int32, spread.shape, 0)
     lane = lax.broadcasted_iota(jnp.int32, spread.shape, 1)
     spread[...] = jnp.where(lax.rem(term, KC) == lane // S, 1.0, 0.0).astype(BF16)
+
+    words.wait()
 
     def list_member(member, total):
         count = meta_ref[member, 0, 2 * SLOTS]
@@ -298,6 +302,17 @@
         grad_out_ref[m * KC : (m + 1) * KC, :] = last_in[m]
 
 
+def store_kernel(mon_ref, flow_ref, mon_hbm, flow_hbm, sems):
+    stores = [
+        pltpu.make_async_copy(mon_ref, mon_hbm, sems.at[0]),
+        pltpu.make_async_copy(flow_ref, flow_hbm, sems.at[1]),
+    ]
+    for store in stores:
+        store.start()
+    for store in stores:
+        store.wait()
+
+
 def vmem(count):
     return [pl.BlockSpec(memory_space=pltpu.VMEM)] * count
 
@@ -343,13 +358,15 @@
             jax.ShapeDtypeStruct(((UNITS + 1) * BLK, S), F32),
             jax.ShapeDtypeStruct((SETS + 1, KC, S), F32),
         ),
-        in_specs=[pl.BlockSpec(memory_space=pltpu.SMEM)] + vmem(4) + [pl.BlockSpec(memory_space=pltpu.HBM)],
+        in_specs=vmem(5) + [pl.BlockSpec(memory_space=pltpu.HBM)],
         out_specs=tuple(vmem(2)),
         scratch_shapes=[
+            pltpu.SMEM((G, 1, S), jnp.int32),
             pltpu.SMEM((G * SLOTS + 8,), jnp.int32),
             pltpu.SMEM((G * SLOTS + 8,), jnp.int32),
             pltpu.SMEM((G * SLOTS + 8,), jnp.int32),
             pltpu.VMEM((1, S), F32),
+            DMA,
             DMA,
             pltpu.VMEM(((UNITS + 1) * BLK, S), F32),
             pltpu.VMEM((UNITS * BLK, S), F32),
@@ -387,6 +404,18 @@
         ),
         name="scatter",
     )(part_mon, part_out)
+    grad_mon, grad_out = pl.pallas_call(
+        store_kernel,
+        out_shape=(
+            jax.ShapeDtypeStruct((OWN, S), F32),
+            jax.ShapeDtypeStruct((SAME * KC, S), F32),
+        ),
+        in_specs=vmem(2),
+        out_specs=tuple([pl.BlockSpec(memory_space=pltpu.HBM)] * 2),
+        scratch_shapes=[DMA((2,))],
+        compiler_params=pltpu.CompilerParams(vmem_limit_bytes=VMEM_BYTES),
+        name="store",
+    )(grad_mon, grad_out)
     return grad_mon, grad_out[None]
 
 

time: 63.7 us -> 63.1 us (level); the launches traced: 63.3 us -> 62 us
  local copies, waits for them, and re-layouts: 1.24 us -> 0 us
    pallas_call x1, Pallas kernels: 19.6 us -> 15.9 us  [local(): pl.pallas_call(tile_kernel, out_shape=(jax.ShapeDtypeStruct(((UNITS + 1)...]
    pallas_call x1, Pallas kernels: 19.3 us -> 22.3 us  [local(): pl.pallas_call(scatter_kernel, out_shape=(jax.ShapeDtypeStruct((OWN, S),...]
    unnamed x2 -> x0, local copies, waits for them, and re-layouts: 1.24 us -> none
    pallas_call x0 -> x1, Pallas kernels: none -> 0.65 us  [local(): pl.pallas_call(store_kernel, out_shape=(jax.ShapeDtypeStruct((OWN, S), F3...]
where the time goes in v6:
time: 63.1 us; the launch traced here: 62 us
  Pallas kernels  60.7 us (96%)
  between operations  1.3 us (2%)
    pallas_call x1, Pallas kernels, local(): pl.pallas_call(scatter_kernel, out_shape=(jax.ShapeDtypeStruct((OWN, S),...  22.3 us
    pallas_call x1, Pallas kernels, local(): pl.pallas_call(gather_kernel, out_shape=(jax.ShapeDtypeStruct((G, SLOTS *...  21.8 us
    pallas_call x1, Pallas kernels, local(): pl.pallas_call(tile_kernel, out_shape=(jax.ShapeDtypeStruct(((UNITS + 1)...  15.9 us

profile of v6, /device:TPU:1, one launch (start us, length us, event | category | flops | bytes accessed | tf_op | source)
XLA Modules:
  0.0 62.0 jit_solution(16790614858896828704)
XLA Ops:
  1.3 21.8 %gather.1 = (bf16[16,64,128]{2,1,0:T(8,128)(2,1)S(1)}, bf16[16,64,128]{2,1,0:T(8,128)(2,1)S(1)}, bf16[4,384,128]{2,1,0:T(8,128)(2,1)S(1)}, f32[4,3,128]{2,1,0:T(4,128)S(1)}, s32[16,1,128]{2,1,0:T(1,128)S(1)}) custom-call(s32[1,1]{1,0:T(1,128)S(6)} %copy.10.count_ref, s32[1,8]{1,0:T(1,128)} %bitcast.10, s32[1,8]{1,0:T(1,128)} %bitcast.11, ...), custom_call_target="tpu_custom_call" | custom-call | tf_op jit(solution)/shard_map/gather/pallas_call | solution.py:329
  23.1 15.9 %tiles.1 = (f32[1664,128]{1,0:T(8,128)S(1)}, f32[129,8,128]{2,1,0:T(8,128)S(1)}) custom-call(s32[16,1,128]{2,1,0:T(1,128)S(1)} %get-tuple-element.13.words_ref, bf16[16,64,128]{2,1,0:T(8,128)(2,1)S(1)} %get-tuple-element.14.tiles_ref, bf16[16,64,128]{2,1,0:T(8,128)(2,1)S(1)} %get-tuple-element.15.flow_ref, ...), custom_call_target="tpu_custom_call" | custom-call | tf_op jit(solution)/shard_map/tiles/pallas_call | solution.py:355
  39.0 22.3 %scatter.1 = (f32[96,128]{1,0:T(8,128)S(1)}, f32[64,128]{1,0:T(8,128)S(1)}) custom-call(f32[1664,128]{1,0:T(8,128)S(1)} %get-tuple-element.18.mon_ref, f32[129,8,128]{2,1,0:T(8,128)S(1)} %get-tuple-element.19.flow_ref), custom_call_target="tpu_custom_call" | custom-call | tf_op jit(solution)/shard_map/scatter/pallas_call | solution.py:384
  61.3 0.7 %store.1 = (f32[96,128]{1,0:T(8,128)}, f32[64,128]{1,0:T(8,128)}) custom-call(f32[96,128]{1,0:T(8,128)S(1)} %get-tuple-element.20.mon_ref, f32[64,128]{1,0:T(8,128)S(1)} %get-tuple-element.21.flow_ref), custom_call_target="tpu_custom_call" | custom-call | tf_op jit(solution)/shard_map/store/pallas_call | solution.py:407

commit v7 on v6

--- a/solution.py
+++ b/solution.py
@@ -28,18 +28,26 @@
 BF16 = jnp.bfloat16
 
 
+def low(value, size):
+    return value & (size - 1)
+
+
+def high(value, size):
+    return value >> (size.bit_length() - 1)
+
+
 def position():
     i = lax.axis_index("mon")
     o = lax.axis_index("out")
-    c = lax.rem(i, NC)
-    z = lax.rem(i // NC, NZ)
-    y = i // (NC * NZ)
-    p = y // 2
-    return o, p, lax.rem(y + p, 2), z, c
+    c = low(i, NC)
+    z = low(high(i, NC), NZ)
+    y = high(i, NC * NZ)
+    p = high(y, 2)
+    return o, p, low(y + p, 2), z, c
 
 
 def at(o, p, e, z, c):
-    y = 2 * p + lax.rem(e + p, 2)
+    y = 2 * p + low(e + p, 2)
     return ((y * NZ + z) * NC + c, o)
 
 
@@ -47,16 +55,16 @@
     own = (c * 2 + e) * NX + o
     group = []
     for d in range(1, G):
-        other = lax.rem(own + d, G)
-        oo, oe, oc = lax.rem(other, NX), lax.rem(other // NX, 2), other // SAME
+        other = low(own + d, G)
+        oo, oe, oc = low(other, NX), low(high(other, NX), 2), high(other, SAME)
         group.append((other, oo, oe, oc, at(oo, p, oe, z, oc)))
     same = []
     for d in range(1, SAME):
-        other = lax.rem(e * NX + o + d, SAME)
-        same.append((other, at(lax.rem(other, NX), p, other // NX, z, c)))
+        other = low(e * NX + o + d, SAME)
+        same.append((other, at(low(other, NX), p, high(other, NX), z, c)))
     along_z = {}
     for d in range(1, NZ):
-        other = lax.rem(z + d, NZ)
+        other = low(z + d, NZ)
         along_z[d] = (other, at(o, p, e, other, c))
     return own, group, same, along_z, at(o, 1 - p, e, z, c)
 
@@ -134,8 +142,8 @@
     for d, (other, _, _, _, device) in enumerate(group):
         rest.append(send(meta_all_ref.at[own], meta_all_ref.at[own], gs.at[1, d], gr.at[1, d], device))
     for d in range(1, 2 * NC):
-        other = lax.rem(unit + d, 2 * NC)
-        device = at(o, p, other // NC, z, lax.rem(other, NC))
+        other = low(unit + d, 2 * NC)
+        device = at(o, p, high(other, NC), z, low(other, NC))
         rest.append(send(mon_all_ref.at[unit], mon_all_ref.at[unit], ms.at[0, d - 1], mr.at[0, d - 1], device))
         rest.append(send(rating_all_ref.at[unit], rating_all_ref.at[unit], ms.at[1, d - 1], mr.at[1, d - 1], device))
     for copy in flows:
@@ -149,7 +157,7 @@
     crossed = [send(block, block, ys.at[0], yr.at[0], across)]
     for d in (1, 7, 2, 6, 3, 5, 4):
         hops[d].wait_recv()
-        block = gathered_ref.at[p * NZ + lax.rem(z + NZ - d, NZ)]
+        block = gathered_ref.at[p * NZ + low(z + NZ - d, NZ)]
         crossed.append(send(block, block, ys.at[d], yr.at[d], across))
     for copy in hops.values():
         copy.wait_send()
@@ -265,7 +273,7 @@
     order = (4, 3, 5, 2, 6, 1, 7, 0)
     crossed = {}
     for d in order:
-        there = pl.ds(((1 - p) * NZ + lax.rem(z + d, NZ)) * SAME, SAME)
+        there = pl.ds(((1 - p) * NZ + low(z + d, NZ)) * SAME, SAME)
         crossed[d] = send(flow_ref.at[there], y_in.at[d], ys.at[d], yr.at[d], across)
     group_hops = []
     for d, (other, oo, oe, oc, device) in enumerate(group):
@@ -273,11 +281,13 @@
         group_hops.append(send(mon_ref.at[rows], mon_in.at[d], gs.at[d], gr.at[d], device))
     hops = []
     for d in order:
-        crossed[d].wait()
-        here = pl.ds((p * NZ + lax.rem(z + d, NZ)) * SAME, SAME)
+        crossed[d].wait_recv()
+        here = pl.ds((p * NZ + low(z + d, NZ)) * SAME, SAME)
         y_sum[d] = flow_ref[here] + y_in[d]
         if d > 0:
             hops.append(send(y_sum.at[d], z_in.at[d - 1], zs.at[d - 1], zr.at[d - 1], along_z[d][1]))
+    for copy in crossed.values():
+        copy.wait_send()
     for copy in hops:
         copy.wait()
     total = y_sum[0]

time: 63.1 us -> 62 us (0.983)
  Pallas kernels: 60.7 us -> 59.9 us
    pallas_call x1, Pallas kernels: 22.3 us -> 18.4 us  [local(): pl.pallas_call(scatter_kernel, out_shape=(jax.ShapeDtypeStruct((OWN, S),...]
    pallas_call x1, Pallas kernels: 15.9 us -> 19.3 us  [local(): pl.pallas_call(tile_kernel, out_shape=(jax.ShapeDtypeStruct(((UNITS + 1)...]
where the time goes in v7:
time: 62 us; the launch traced here: 61.2 us
  Pallas kernels  59.9 us (97%)
  between operations  1.3 us (2%)
    pallas_call x1, Pallas kernels, local(): pl.pallas_call(gather_kernel, out_shape=(jax.ShapeDtypeStruct((G, SLOTS *...  21.6 us
    pallas_call x1, Pallas kernels, local(): pl.pallas_call(tile_kernel, out_shape=(jax.ShapeDtypeStruct(((UNITS + 1)...  19.3 us
    pallas_call x1, Pallas kernels, local(): pl.pallas_call(scatter_kernel, out_shape=(jax.ShapeDtypeStruct((OWN, S),...  18.4 us

profile of v7, /device:TPU:1, one launch (start us, length us, event | category | flops | bytes accessed | tf_op | source)
XLA Modules:
  0.0 61.2 jit_solution(14730991033726857612)
XLA Ops:
  1.3 21.6 %gather.1 = (bf16[16,64,128]{2,1,0:T(8,128)(2,1)S(1)}, bf16[16,64,128]{2,1,0:T(8,128)(2,1)S(1)}, bf16[4,384,128]{2,1,0:T(8,128)(2,1)S(1)}, f32[4,3,128]{2,1,0:T(4,128)S(1)}, s32[16,1,128]{2,1,0:T(1,128)S(1)}) custom-call(s32[1,1]{1,0:T(1,128)S(6)} %copy.10.count_ref, s32[1,8]{1,0:T(1,128)} %bitcast.10, s32[1,8]{1,0:T(1,128)} %bitcast.11, ...), custom_call_target="tpu_custom_call" | custom-call | tf_op jit(solution)/shard_map/gather/pallas_call | solution.py:339
  22.9 19.3 %tiles.1 = (f32[1664,128]{1,0:T(8,128)S(1)}, f32[129,8,128]{2,1,0:T(8,128)S(1)}) custom-call(s32[16,1,128]{2,1,0:T(1,128)S(1)} %get-tuple-element.13.words_ref, bf16[16,64,128]{2,1,0:T(8,128)(2,1)S(1)} %get-tuple-element.14.tiles_ref, bf16[16,64,128]{2,1,0:T(8,128)(2,1)S(1)} %get-tuple-element.15.flow_ref, ...), custom_call_target="tpu_custom_call" | custom-call | tf_op jit(solution)/shard_map/tiles/pallas_call | solution.py:365
  42.1 18.4 %scatter.1 = (f32[96,128]{1,0:T(8,128)S(1)}, f32[64,128]{1,0:T(8,128)S(1)}) custom-call(f32[1664,128]{1,0:T(8,128)S(1)} %get-tuple-element.18.mon_ref, f32[129,8,128]{2,1,0:T(8,128)S(1)} %get-tuple-element.19.flow_ref), custom_call_target="tpu_custom_call" | custom-call | tf_op jit(solution)/shard_map/scatter/pallas_call | solution.py:394
  60.6 0.7 %store.1 = (f32[96,128]{1,0:T(8,128)}, f32[64,128]{1,0:T(8,128)}) custom-call(f32[96,128]{1,0:T(8,128)S(1)} %get-tuple-element.20.mon_ref, f32[64,128]{1,0:T(8,128)S(1)} %get-tuple-element.21.flow_ref), custom_call_target="tpu_custom_call" | custom-call | tf_op jit(solution)/shard_map/store/pallas_call | solution.py:417

commit v8 on v7

--- a/solution.py
+++ b/solution.py
@@ -275,10 +275,9 @@
     for d in order:
         there = pl.ds(((1 - p) * NZ + low(z + d, NZ)) * SAME, SAME)
         crossed[d] = send(flow_ref.at[there], y_in.at[d], ys.at[d], yr.at[d], across)
-    group_hops = []
     for d, (other, oo, oe, oc, device) in enumerate(group):
         rows = pl.ds(pl.multiple_of((oe * NC + oc) * MB * BLK + oo * OWN, 8), OWN)
-        group_hops.append(send(mon_ref.at[rows], mon_in.at[d], gs.at[d], gr.at[d], device))
+        send(mon_ref.at[rows], mon_in.at[d], gs, gr, device)
     hops = []
     for d in order:
         crossed[d].wait_recv()
@@ -299,8 +298,8 @@
         send(z_sum.at[other], last_in.at[place], fs.at[d], fr.at[d], device)
         for d, (other, device) in enumerate(same)
     ]
-    for copy in group_hops:
-        copy.wait()
+    for sem in (gs, gr):
+        pltpu.make_async_copy(mon_in, mon_in, sem).wait()
     rows = pl.ds(pl.multiple_of((e * NC + c) * MB * BLK + o * OWN, 8), OWN)
     total = mon_ref[rows, :]
     for d in range(G - 1):
@@ -406,7 +405,7 @@
             pltpu.VMEM((NZ - 1, SAME, KC, S), F32),
             pltpu.VMEM((SAME, KC, S), F32),
             pltpu.VMEM((SAME, KC, S), F32),
-            DMA((G - 1,)), DMA((G - 1,)), DMA((SAME - 1,)), DMA((SAME - 1,)),
+            DMA, DMA, DMA((SAME - 1,)), DMA((SAME - 1,)),
             DMA((NZ - 1,)), DMA((NZ - 1,)), DMA((NZ,)), DMA((NZ,)),
         ],
         compiler_params=pltpu.CompilerParams(

time: 62 us -> 62.6 us (level)
    pallas_call x1, Pallas kernels: 18.4 us -> 23.8 us  [local(): pl.pallas_call(scatter_kernel, out_shape=(jax.ShapeDtypeStruct((OWN, S),...]
    pallas_call x1, Pallas kernels: 19.3 us -> 14.3 us  [local(): pl.pallas_call(tile_kernel, out_shape=(jax.ShapeDtypeStruct(((UNITS + 1)...]
where the time goes in v8:
time: 62.6 us; the launch traced here: 61.7 us
  Pallas kernels  60.4 us (96%)
  between operations  1.3 us (2%)
    pallas_call x1, Pallas kernels, local(): pl.pallas_call(scatter_kernel, out_shape=(jax.ShapeDtypeStruct((OWN, S),...  23.8 us
    pallas_call x1, Pallas kernels, local(): pl.pallas_call(gather_kernel, out_shape=(jax.ShapeDtypeStruct((G, SLOTS *...  21.6 us
    pallas_call x1, Pallas kernels, local(): pl.pallas_call(tile_kernel, out_shape=(jax.ShapeDtypeStruct(((UNITS + 1)...  14.3 us

profile of v8, /device:TPU:1, one launch (start us, length us, event | category | flops | bytes accessed | tf_op | source)
XLA Modules:
  0.0 61.7 jit_solution(6596191548598977711)
XLA Ops:
  1.3 21.6 %gather.1 = (bf16[16,64,128]{2,1,0:T(8,128)(2,1)S(1)}, bf16[16,64,128]{2,1,0:T(8,128)(2,1)S(1)}, bf16[4,384,128]{2,1,0:T(8,128)(2,1)S(1)}, f32[4,3,128]{2,1,0:T(4,128)S(1)}, s32[16,1,128]{2,1,0:T(1,128)S(1)}) custom-call(s32[1,1]{1,0:T(1,128)S(6)} %copy.10.count_ref, s32[1,8]{1,0:T(1,128)} %bitcast.10, s32[1,8]{1,0:T(1,128)} %bitcast.11, ...), custom_call_target="tpu_custom_call" | custom-call | tf_op jit(solution)/shard_map/gather/pallas_call | solution.py:338
  22.9 14.3 %tiles.1 = (f32[1664,128]{1,0:T(8,128)S(1)}, f32[129,8,128]{2,1,0:T(8,128)S(1)}) custom-call(s32[16,1,128]{2,1,0:T(1,128)S(1)} %get-tuple-element.13.words_ref, bf16[16,64,128]{2,1,0:T(8,128)(2,1)S(1)} %get-tuple-element.14.tiles_ref, bf16[16,64,128]{2,1,0:T(8,128)(2,1)S(1)} %get-tuple-element.15.flow_ref, ...), custom_call_target="tpu_custom_call" | custom-call | tf_op jit(solution)/shard_map/tiles/pallas_call | solution.py:364
  37.2 23.8 %scatter.1 = (f32[96,128]{1,0:T(8,128)S(1)}, f32[64,128]{1,0:T(8,128)S(1)}) custom-call(f32[1664,128]{1,0:T(8,128)S(1)} %get-tuple-element.18.mon_ref, f32[129,8,128]{2,1,0:T(8,128)S(1)} %get-tuple-element.19.flow_ref), custom_call_target="tpu_custom_call" | custom-call | tf_op jit(solution)/shard_map/scatter/pallas_call | solution.py:393
  61.0 0.7 %store.1 = (f32[96,128]{1,0:T(8,128)}, f32[64,128]{1,0:T(8,128)}) custom-call(f32[96,128]{1,0:T(8,128)S(1)} %get-tuple-element.20.mon_ref, f32[64,128]{1,0:T(8,128)S(1)} %get-tuple-element.21.flow_ref), custom_call_target="tpu_custom_call" | custom-call | tf_op jit(solution)/shard_map/store/pallas_call | solution.py:416

commit v9 on v8

--- a/solution.py
+++ b/solution.py
@@ -295,7 +295,7 @@
     z_sum[...] = total
     last_in[place] = z_sum[place]
     hops = [
-        send(z_sum.at[other], last_in.at[place], fs.at[d], fr.at[d], device)
+        send(z_sum.at[other], last_in.at[place], fs, fr, device)
         for d, (other, device) in enumerate(same)
     ]
     for sem in (gs, gr):
@@ -305,8 +305,9 @@
     for d in range(G - 1):
         total = total + mon_in[d]
     grad_mon_ref[...] = total
-    for copy in hops:
-        copy.wait()
+    most = last_in.at[pl.ds(0, SAME - 1)]
+    for sem in (fs, fr):
+        pltpu.make_async_copy(most, most, sem).wait()
     for m in range(SAME):
         grad_out_ref[m * KC : (m + 1) * KC, :] = last_in[m]
 
@@ -405,7 +406,7 @@
             pltpu.VMEM((NZ - 1, SAME, KC, S), F32),
             pltpu.VMEM((SAME, KC, S), F32),
             pltpu.VMEM((SAME, KC, S), F32),
-            DMA, DMA, DMA((SAME - 1,)), DMA((SAME - 1,)),
+            DMA, DMA, DMA, DMA,
             DMA((NZ - 1,)), DMA((NZ - 1,)), DMA((NZ,)), DMA((NZ,)),
         ],
         compiler_params=pltpu.CompilerParams(

time: 62.6 us -> 64.2 us (1.026)
  the two profiles are of different devices: /device:TPU:1 before, /device:TPU:16 now
where the time goes in v9:
time: 64.2 us; the launch traced here: 63.6 us
  Pallas kernels  62.3 us (97%)
  between operations  1.3 us (2%)
    pallas_call x1, Pallas kernels, local(): pl.pallas_call(scatter_kernel, out_shape=(jax.ShapeDtypeStruct((OWN, S),...  22 us
    pallas_call x1, Pallas kernels, local(): pl.pallas_call(gather_kernel, out_shape=(jax.ShapeDtypeStruct((G, SLOTS *...  21.1 us
    pallas_call x1, Pallas kernels, local(): pl.pallas_call(tile_kernel, out_shape=(jax.ShapeDtypeStruct(((UNITS + 1)...  18.5 us

profile of v9, /device:TPU:16, one launch (start us, length us, event | category | flops | bytes accessed | tf_op | source)
XLA Modules:
  0.0 63.6 jit_solution(16991266916686994713)
XLA Ops:
  1.3 21.1 %gather.1 = (bf16[16,64,128]{2,1,0:T(8,128)(2,1)S(1)}, bf16[16,64,128]{2,1,0:T(8,128)(2,1)S(1)}, bf16[4,384,128]{2,1,0:T(8,128)(2,1)S(1)}, f32[4,3,128]{2,1,0:T(4,128)S(1)}, s32[16,1,128]{2,1,0:T(1,128)S(1)}) custom-call(s32[1,1]{1,0:T(1,128)S(6)} %copy.10.count_ref, s32[1,8]{1,0:T(1,128)} %bitcast.10, s32[1,8]{1,0:T(1,128)} %bitcast.11, ...), custom_call_target="tpu_custom_call" | custom-call | tf_op jit(solution)/shard_map/gather/pallas_call | solution.py:339
  22.4 18.5 %tiles.1 = (f32[1664,128]{1,0:T(8,128)S(1)}, f32[129,8,128]{2,1,0:T(8,128)S(1)}) custom-call(s32[16,1,128]{2,1,0:T(1,128)S(1)} %get-tuple-element.13.words_ref, bf16[16,64,128]{2,1,0:T(8,128)(2,1)S(1)} %get-tuple-element.14.tiles_ref, bf16[16,64,128]{2,1,0:T(8,128)(2,1)S(1)} %get-tuple-element.15.flow_ref, ...), custom_call_target="tpu_custom_call" | custom-call | tf_op jit(solution)/shard_map/tiles/pallas_call | solution.py:365
  40.9 22.0 %scatter.1 = (f32[96,128]{1,0:T(8,128)S(1)}, f32[64,128]{1,0:T(8,128)S(1)}) custom-call(f32[1664,128]{1,0:T(8,128)S(1)} %get-tuple-element.18.mon_ref, f32[129,8,128]{2,1,0:T(8,128)S(1)} %get-tuple-element.19.flow_ref), custom_call_target="tpu_custom_call" | custom-call | tf_op jit(solution)/shard_map/scatter/pallas_call | solution.py:394
  63.0 0.7 %store.1 = (f32[96,128]{1,0:T(8,128)}, f32[64,128]{1,0:T(8,128)}) custom-call(f32[96,128]{1,0:T(8,128)S(1)} %get-tuple-element.20.mon_ref, f32[64,128]{1,0:T(8,128)S(1)} %get-tuple-element.21.flow_ref), custom_call_target="tpu_custom_call" | custom-call | tf_op jit(solution)/shard_map/store/pallas_call | solution.py:417
